TPU v7x, 512 devices: a whole 4x8x8 slice. The times are simulated.
512 devices in a mesh: col: 128 (over y, z, core), lev: 4 (over x).
Axes of the slice: x: 4, y: 8, z: 8, core: 2. Of those that a mesh axis runs over, the one named last changes fastest.
Arguments:
- fields: bfloat16 [2, 32, 131072], P(None, 'lev', 'col'), may hold values from 0.5 to 3
- bracket: int32 [8, 131072], P(None, 'col'), may hold values from 0 to 30
- fraction: float32 [8, 131072], P(None, 'col'), may hold values from 0 to 1
- remap_weights: bfloat16 [2048, 128, 128], P('col'), may hold values from 0 to 0.015625
- intersections: int32 [3, 4096], P(None, 'col'), may hold values from 0 to 1023, as said below
- tile_owner: int32 [1024], replicated, may hold values from 0 to 1023, as said below
Outputs:
- normalized: float32 [2, 8, 1024, 128], P(None, 'lev', 'col')
Inputs may be any that keep to these rules, and one draw needn't show every extreme that they name: `intersections`: row 0 names a source block of the entry's own col index; row 1 a target tile whose owner, tile_owner[tile] // 8, lies within 2 indices of the entry's col index or exactly 64 indices away, cyclically; row 2 a weight block of the entry's own col index. `tile_owner`: A permutation of the tiles.
All inputs are finite; a program needn't handle non-finite values.
Results may differ from a plain program's by a relative error of at most 0.00031.
Values may be sent and summed in bfloat16 or wider, within the bound.
No kernel may reach another device: no remote copies, remote signals or barrier semaphores. Data moves between devices by JAX's collectives and lax.ppermute only.
A program may use at most 64 MiB of HBM per device.

v0:
```python
import jax
import jax.numpy as jnp
from jax import lax
from jax.sharding import PartitionSpec as P

F = 2
PLEV = 8


epsilon = 1e-06


def mix_levels(level_block, lower_level, weight_up):
    level_ids = jnp.arange(level_block.shape[1], dtype=jnp.int32)
    is_below = level_ids[None, :, None] == lower_level[:, None, :]
    is_above = level_ids[None, :, None] == lower_level[:, None, :] + 1
    level_coef = jnp.where(
        is_below, 1.0 - weight_up[:, None, :], jnp.where(is_above, weight_up[:, None, :], 0.0)
    )
    return jnp.sum(level_coef[None] * level_block.astype(jnp.float32)[:, None], axis=2)


def gather_rows(selector, partial_tiles):
    return lax.dot_general(
        selector,
        partial_tiles,
        (((0,), (0,)), ((), ())),
        precision=lax.Precision.HIGHEST,
        preferred_element_type=jnp.float32,
    )


def per_device(fields, bracket, fraction, remap_weights, intersections, tile_owner):
    lev_index = lax.axis_index("lev")
    plev_dev = PLEV // lax.axis_size("lev")
    column_levels = lax.all_gather(fields, "lev", axis=1, tiled=True)
    lower_level = lax.dynamic_slice_in_dim(bracket, lev_index * plev_dev, plev_dev, 0)
    weight_up = lax.dynamic_slice_in_dim(fraction, lev_index * plev_dev, plev_dev, 0)
    interp = mix_levels(column_levels, lower_level, weight_up).astype(jnp.bfloat16)
    block_cols = remap_weights.shape[1]
    tile_cells = remap_weights.shape[2]
    blocks = interp.reshape(F, plev_dev, -1, block_cols)
    chosen = jnp.take(blocks, intersections[0], axis=2)
    picked = jnp.take(remap_weights, intersections[2], axis=0)
    partial_tiles = jnp.einsum("fpeb,ebt->efpt", chosen, picked, preferred_element_type=jnp.float32)
    entries = partial_tiles.shape[0]
    partial_tiles = partial_tiles.reshape(entries, -1)
    tile_total = tile_owner.shape[0]
    col_count = lax.axis_size("col")
    tile_dev = tile_total // col_count
    matches = intersections[1][:, None] == jnp.arange(tile_total, dtype=jnp.int32)[None, :]
    slot_index = jnp.sum(jnp.where(matches, tile_owner[None, :], 0), axis=1)
    selector = (
        slot_index[:, None] == jnp.arange(tile_dev * lax.axis_size("col"), dtype=jnp.int32)[None, :]
    ).astype(jnp.float32)
    remapped = lax.psum_scatter(
        gather_rows(selector, partial_tiles), "col", scatter_dimension=0, tiled=True
    )
    remapped = remapped.reshape(tile_dev, F, plev_dev, tile_cells).transpose(1, 2, 0, 3)
    shifted_left = jnp.concatenate([remapped[..., :1], remapped[..., :-1]], axis=-1)
    shifted_right = jnp.concatenate([remapped[..., 1:], remapped[..., -1:]], axis=-1)
    filtered = 0.25 * shifted_left + 0.5 * remapped + 0.25 * shifted_right
    cells = float(tile_dev * tile_cells * col_count)
    local_sums = jnp.sum(filtered, axis=(2, 3))
    field_mean = lax.psum(local_sums, "col") / cells
    centered = filtered - field_mean[:, :, None, None]
    field_var = lax.psum(jnp.sum(centered * centered, axis=(2, 3)), "col") / cells
    return centered * lax.rsqrt(field_var + epsilon)[:, :, None, None]


def solution(mesh):
    in_specs = (
        P(None, "lev", "col"),
        P(None, "col"),
        P(None, "col"),
        P("col", None, None),
        P(None, "col"),
        P(),
    )
    out_specs = P(None, "lev", "col", None)
    return jax.shard_map(
        per_device, mesh=mesh, in_specs=in_specs, out_specs=out_specs, check_vma=False
    )
```

profile of v0, /device:TPU:1, one launch (start us, length us, event | category | flops | bytes accessed | tf_op | source)
XLA Modules:
  0.0 736.7 jit_solution(11726878282647201093)
XLA Ops:
  6.5 0.0 copy-start
  6.5 0.7 slice_bitcast_fusion
  7.3 0.8 fusion.11
  8.0 0.8 compare_and_fusion.1
  8.8 0.8 broadcast_add_fusion
  9.6 0.8 broadcast_subtract_fusion
  10.3 10.5 %all_gather.3 = bf16[2,32,1024]{2,1,0:T(8,128)(2,1)S(1)} all-gather(bf16[2,8,1024]{2,1,0:T(8,128)(2,1)} %param.6), channel_id=1, replica_groups=mesh['col'=128,'lev'=4] {'lev'}, dimensions={1}, use_global_device_ids=true | all-gather | bytes 163840 | tf_op jit(solution)/shard_map/all_gather | solution.py:36
  20.9 0.1 multiply_reduce_fusion
  21.0 0.0 copy-start.1
  21.0 0.6 gather_fusion
  21.6 0.7 gather_fusion.1
  22.4 0.5 fusion
  22.9 0.1 reshape.97
  22.9 0.2 select_reduce_fusion
  23.1 2.5 fusion.5
  25.6 0.0 reduce-scatter.2.cloned.1.call-update
  25.6 202.3 %reduce-scatter.2.cloned.1.call-done = f32[8,512]{1,0:T(8,128)} async-done(((f32[1024,512]{1,0:T(8,128)}), f32[8,512]{1,0:T(8,128)}) %reduce-scatter.2.cloned.1.call-update) | async-done | bytes 16400 | tf_op jit(solution)/shard_map/reduce_scatter | solution.py:56
  227.9 0.9 fusion.17
  228.8 0.9 fusion.16
  229.6 0.9 fusion.14
  230.5 251.6 %psum.14 = f32[2,2]{1,0:T(2,128)S(1)} all-reduce(f32[2,2]{1,0:T(2,128)S(1)} %get-tuple-element.5), channel_id=1, replica_groups=mesh['col'=128,'lev'=4] {'col'}, use_global_device_ids=true, to_apply=%region_4.5 | all-reduce | flops 4 | bytes 32 | tf_op jit(solution)/shard_map/psum | solution.py:65
  482.2 0.2 multiply_reduce_fusion.1
  482.3 246.8 %psum.15 = f32[2,2]{1,0:T(2,128)S(1)} all-reduce(f32[2,2]{1,0:T(2,128)S(1)} %multiply_reduce_fusion.1), channel_id=1, replica_groups=mesh['col'=128,'lev'=4] {'col'}, use_global_device_ids=true, to_apply=%region_6.7 | all-reduce | flops 4 | bytes 32 | tf_op jit(solution)/shard_map/psum | solution.py:67
  729.1 0.7 subtract_multiply_fusion
  (8 shorter events, 0.1 us)
Async XLA Ops:
  6.5 15.1 %copy-start = (bf16[16,128,128]{2,1,0:T(8,128)(2,1)S(1)}, bf16[16,128,128]{2,1,0:T(8,128)(2,1)}, u32[]{:S(2)}) copy-start(bf16[16,128,128]{2,1,0:T(8,128)(2,1)} %param.9) | copy-start | bytes 1572868
  6.5 221.4 %reduce-scatter.2.cloned.1.call-start = ((), (), s32[]{:S(2)}) async-start(), calls=%async_computation.1 | async-start | bytes 2113536 | tf_op jit(solution)/shard_map/reduce_scatter | solution.py:56
  21.0 1.9 copy-start.1
Sparse Core Ops, SparseCore 0:
  25.7 202.1 reduce-scatter.1
where the time goes:
time: 737 us
  blocking collectives  509 us (69%)
  waiting for transfers between devices  202 us (27%)
  between operations  13.5 us (2%)
    psum x1, blocking collectives, per_device(): field_mean = lax.psum(local_sums, 'col') / cells  252 us
    psum x1, blocking collectives, per_device(): lax.psum(jnp.sum(centered * centered, axis=(2, 3)), 'col') / cells  247 us
    reduce_scatter x1, waiting for transfers between devices, per_device(): lax.psum_scatter(gather_rows(selector, partial_tiles), 'col', scatter_dim...  202 us
  transfers between devices with their start and end apart: 1, of which 1 were waited for; matrix products, arithmetic and copies ran while one was open for 0% of the time, Pallas kernels for 0%

commit v1 on v0

v1 whole, which is shorter than its diff:
```python
import jax
import jax.numpy as jnp
from jax import lax
from jax.experimental import pallas as pl
from jax.experimental.pallas import tpu as pltpu
from jax.sharding import PartitionSpec as P

F = 2
PLEV = 8
GROUP = 4
CROSS = 2

epsilon = 1e-06


def mix_kernel(fields_ref, bracket_ref, fraction_ref, out_ref):
    levels = fields_ref.shape[1]
    lev_dev, rows, blocks, cols = out_ref.shape
    plev_dev = rows // F
    lower = bracket_ref[...] - lax.axis_index("lev") * levels
    up = fraction_ref[...]
    down = 1.0 - up
    acc = [jnp.zeros(up.shape, jnp.float32) for _ in range(F)]
    for k in range(levels):
        coef = jnp.where(lower == k, down, jnp.where(lower == k - 1, up, 0.0))
        for f in range(F):
            acc[f] = acc[f] + coef * fields_ref[f, k : k + 1, :].astype(jnp.float32)
    for f in range(F):
        for p in range(lev_dev * plev_dev):
            for s in range(blocks):
                out_ref[p // plev_dev, f * plev_dev + p % plev_dev, s : s + 1, :] = acc[f][
                    p : p + 1, s * cols : (s + 1) * cols
                ]


def count_kernel(intersections_ref, owner_ref, out_ref):
    rows, pairs = out_ref.shape
    entries = intersections_ref.shape[1]
    tile_rows, lanes = owner_ref.shape
    blocks = 8
    tile_dev = 8
    me = lax.axis_index("col")
    col_count = tile_rows * lanes // tile_dev
    eye = lax.broadcasted_iota(jnp.int32, (entries, entries), 0) == lax.broadcasted_iota(
        jnp.int32, (entries, entries), 1
    )

    def column(row):
        return jnp.sum(jnp.where(eye, row, 0.0), axis=1, keepdims=True)

    def lane_row(col):
        return jnp.sum(jnp.where(eye, col, 0.0), axis=0, keepdims=True)

    table = intersections_ref[...].astype(jnp.float32)
    source = column(table[0:1])
    target = column(table[1:2])
    weight = column(table[2:3])
    owner = owner_ref[...].astype(jnp.float32)
    lane = lax.broadcasted_iota(jnp.int32, (entries, lanes), 1).astype(jnp.float32)
    found = jnp.zeros((entries, lanes), jnp.float32)
    for r in range(tile_rows):
        found = found + jnp.where(target == lane + float(r * lanes), owner[r : r + 1], 0.0)
    slot = jnp.sum(found, axis=1, keepdims=True)
    slot = lane_row(slot).astype(jnp.int32)
    dev = slot // tile_dev
    local = slot % tile_dev
    far = dev == (me + col_count // 2) % col_count
    same = dev // GROUP == me // GROUP
    block = jnp.where(same, dev % GROUP, jnp.where(far, GROUP + CROSS, GROUP + dev % CROSS))
    row = block * tile_dev + local
    rows_hit = lax.broadcasted_iota(jnp.int32, (rows, entries), 0) == row
    pair = weight * float(blocks) + source
    pair_hit = lax.broadcasted_iota(jnp.int32, (entries, pairs), 1).astype(jnp.float32) == pair
    out_ref[...] = jnp.dot(
        jnp.where(rows_hit, 1.0, 0.0).astype(jnp.bfloat16),
        jnp.where(pair_hit, 1.0, 0.0).astype(jnp.bfloat16),
        preferred_element_type=jnp.float32,
    )


def remap_kernel(mixed_ref, weights_ref, counts_ref, group_ref, cross_ref, far_ref, parts_ref):
    lev_dev, rows, blocks, cols = mixed_ref.shape
    cells = weights_ref.shape[2]
    interp = mixed_ref[0]
    for k in range(1, lev_dev):
        interp = interp + mixed_ref[k]
    interp = interp.reshape(rows * blocks, cols).astype(jnp.bfloat16)
    for w in range(weights_ref.shape[0]):
        part = jnp.dot(interp, weights_ref[w], preferred_element_type=jnp.float32)
        for r in range(rows):
            parts_ref[w * blocks : (w + 1) * blocks, r * cells : (r + 1) * cells] = part[
                r * blocks : (r + 1) * blocks
            ]
    counts = counts_ref[...].astype(jnp.bfloat16)
    parts = parts_ref[...]
    high = parts.astype(jnp.bfloat16)
    rest = parts - high.astype(jnp.float32)
    middle = rest.astype(jnp.bfloat16)
    low = (rest - middle.astype(jnp.float32)).astype(jnp.bfloat16)
    total = (
        jnp.dot(counts, low, preferred_element_type=jnp.float32)
        + jnp.dot(counts, middle, preferred_element_type=jnp.float32)
        + jnp.dot(counts, high, preferred_element_type=jnp.float32)
    )
    n_group = group_ref.shape[0]
    n_cross = cross_ref.shape[0]
    group_ref[...] = total[:n_group]
    cross_ref[...] = total[n_group : n_group + n_cross]
    far_ref[...] = total[n_group + n_cross :]


def join_kernel(group_ref, cross_ref, out_ref):
    half = cross_ref.shape[0]
    upper = (lax.axis_index("col") % GROUP) >= CROSS
    cross = cross_ref[...]
    out_ref[:half] = group_ref[:half] + jnp.where(upper, 0.0, cross)
    out_ref[half:] = group_ref[half:] + jnp.where(upper, cross, 0.0)


def filter_kernel(near_ref, far_ref, filtered_ref, stats_ref):
    tile_dev = far_ref.shape[0]
    rows = filtered_ref.shape[0]
    cells = filtered_ref.shape[2]
    total = far_ref[...]
    for k in range(near_ref.shape[0] // tile_dev):
        total = total + near_ref[k * tile_dev : (k + 1) * tile_dev]
    lane = lax.broadcasted_iota(jnp.int32, (1, cells), 1)
    stats = jnp.zeros((1, cells), jnp.float32)
    for r in range(rows):
        x = total[:, r * cells : (r + 1) * cells]
        left = jnp.concatenate([x[:, :1], x[:, :-1]], axis=1)
        right = jnp.concatenate([x[:, 1:], x[:, -1:]], axis=1)
        y = 0.25 * left + 0.5 * x + 0.25 * right
        filtered_ref[r] = y
        mean = jnp.sum(jnp.sum(y, axis=0, keepdims=True), axis=1, keepdims=True) / float(tile_dev * cells)
        off = y - mean
        spread = jnp.sum(jnp.sum(off * off, axis=0, keepdims=True), axis=1, keepdims=True)
        stats = jnp.where(lane == r, mean, jnp.where(lane == rows + r, spread, stats))
    stats_ref[...] = jnp.broadcast_to(stats[None], stats_ref.shape)


def per_device(fields, bracket, fraction, remap_weights, intersections, tile_owner):
    lev_dev = lax.axis_size("lev")
    col_count = lax.axis_size("col")
    plev_dev = PLEV // lev_dev
    weights_dev, block_cols, tile_cells = remap_weights.shape
    blocks = fields.shape[2] // block_cols
    tile_dev = tile_owner.shape[0] // col_count
    rows = F * plev_dev
    f32 = jnp.float32

    mixed = pl.pallas_call(
        mix_kernel,
        out_shape=jax.ShapeDtypeStruct((lev_dev, rows, blocks, block_cols), f32),
        name="mix_levels",
    )(fields, bracket, fraction)
    mixed = lax.all_to_all(mixed, "lev", 0, 0, tiled=True)

    n_group = GROUP * tile_dev
    n_cross = CROSS * tile_dev
    counts = pl.pallas_call(
        count_kernel,
        out_shape=jax.ShapeDtypeStruct((n_group + n_cross + tile_dev, weights_dev * blocks), f32),
        name="count_entries",
    )(intersections, tile_owner.reshape(-1, 128))
    group, cross, far = pl.pallas_call(
        remap_kernel,
        out_shape=[
            jax.ShapeDtypeStruct((n, rows * tile_cells), f32) for n in (n_group, n_cross, tile_dev)
        ],
        scratch_shapes=[pltpu.VMEM((weights_dev * blocks, rows * tile_cells), f32)],
        name="remap_blocks",
    )(mixed, remap_weights, counts)

    swap = [
        (d, (d - CROSS) % col_count if d % GROUP < CROSS else (d + CROSS) % col_count)
        for d in range(col_count)
    ]
    opposite = [(d, (d + col_count // 2) % col_count) for d in range(col_count)]
    groups = [[g * GROUP + k for k in range(GROUP)] for g in range(col_count // GROUP)]
    far = lax.ppermute(far, "col", opposite)
    cross = lax.ppermute(cross, "col", swap)
    near = pl.pallas_call(
        join_kernel,
        out_shape=jax.ShapeDtypeStruct((n_group, rows * tile_cells), f32),
        name="join_forwarded",
    )(group, cross)
    near = lax.all_to_all(near, "col", 0, 0, tiled=True, axis_index_groups=groups)

    filtered, stats = pl.pallas_call(
        filter_kernel,
        out_shape=[
            jax.ShapeDtypeStruct((rows, tile_dev, tile_cells), f32),
            jax.ShapeDtypeStruct((col_count, 1, tile_cells), f32),
        ],
        name="filter_tiles",
    )(near, far)
    stats = lax.all_to_all(stats, "col", 0, 0, tiled=True)[:, 0]
    count = float(tile_dev * tile_cells)
    field_mean = jnp.sum(stats[:, :rows], axis=0) / float(col_count)
    apart = stats[:, :rows] - field_mean[None]
    spread = jnp.sum(stats[:, rows : 2 * rows] + count * apart * apart, axis=0)
    field_var = spread / (count * col_count)
    scale = lax.rsqrt(field_var + epsilon)
    normalized = (filtered - field_mean[:, None, None]) * scale[:, None, None]
    return normalized.reshape(F, plev_dev, tile_dev, tile_cells)


def solution(mesh):
    in_specs = (
        P(None, "lev", "col"),
        P(None, "col"),
        P(None, "col"),
        P("col", None, None),
        P(None, "col"),
        P(),
    )
    out_specs = P(None, "lev", "col", None)
    return jax.shard_map(
        per_device, mesh=mesh, in_specs=in_specs, out_specs=out_specs, check_vma=False
    )
```

time: 737 us -> 71.9 us (0.10)
  blocking collectives: 509 us -> 21.9 us
  waiting for transfers between devices: 202 us -> 8.3 us
  starting transfers between devices: 0.01 us -> 29.2 us
  between operations: 13.5 us -> 0.03 us
  Pallas kernels: 0 us -> 8.5 us
    psum x2 -> x0, blocking collectives: 498 us -> none  [the longest x1 252 us: per_device(): field_mean = lax.psum(local_sums, 'col') / cells]
    reduce_scatter x1 -> x0, waiting for transfers between devices: 202 us -> none  [per_device(): lax.psum_scatter(gather_rows(selector, partial_tiles), 'col', scatter_dim...]
    all_to_all x0 -> x1, blocking collectives: none -> 21.9 us  [per_device(): stats = lax.all_to_all(stats, 'col', 0, 0, tiled=True)[:, 0]]
    ppermute x0 -> x2, starting transfers between devices: none -> 18 us  [the longest x1 13.6 us: per_device(): cross = lax.ppermute(cross, 'col', swap)]
    all_to_all x0 -> x2, starting transfers between devices: none -> 11.2 us  [the longest x1 6.35 us: per_device(): lax.all_to_all(near, 'col', 0, 0, tiled=True, axis_index_groups=groups)]
    all_gather x1 -> x0, blocking collectives: 10.5 us -> none  [per_device(): column_levels = lax.all_gather(fields, 'lev', axis=1, tiled=True)]
    pallas_call x0 -> x5, Pallas kernels: none -> 8.5 us  [the longest x1 2.11 us: per_device(): pl.pallas_call(remap_kernel, out_shape=[jax.ShapeDtypeStruct((n, rows * t...]
  transfers between devices with their start and end apart: 1 -> 4, of which waited for: 1 -> 3; matrix products, arithmetic and copies ran while one was open for 0% -> 0% of each run, Pallas kernels for 0% -> 2%
where the time goes in v1:
time: 71.9 us; the launch traced here: 71.2 us
  starting transfers between devices  29.2 us (41%)
  blocking collectives  21.9 us (30%)
  Pallas kernels  8.5 us (12%)
  waiting for transfers between devices  8.3 us (12%)
  local copies, waits for them, and re-layouts  2.48 us (3%)
  other arithmetic  0.83 us (1%)
    all_to_all x1, blocking collectives, per_device(): stats = lax.all_to_all(stats, 'col', 0, 0, tiled=True)[:, 0]  21.9 us
    ppermute x1, starting transfers between devices, per_device(): cross = lax.ppermute(cross, 'col', swap)  13.6 us
    all_to_all x1, starting transfers between devices, per_device(): lax.all_to_all(near, 'col', 0, 0, tiled=True, axis_index_groups=groups)  6.35 us
    all_to_all x1, starting transfers between devices, per_device(): mixed = lax.all_to_all(mixed, 'lev', 0, 0, tiled=True)  4.83 us
    ppermute x1, starting transfers between devices, per_device(): far = lax.ppermute(far, 'col', opposite)  4.42 us
    ppermute x1, waiting for transfers between devices, per_device(): far = lax.ppermute(far, 'col', opposite)  3.95 us
    all_to_all x1, waiting for transfers between devices, per_device(): mixed = lax.all_to_all(mixed, 'lev', 0, 0, tiled=True)  2.85 us
    unnamed x12, local copies, waits for them, and re-layouts  2.48 us
  transfers between devices with their start and end apart: 4, of which 3 were waited for; matrix products, arithmetic and copies ran while one was open for 0% of the time, Pallas kernels for 2%

profile of v1, /device:TPU:1, one launch (start us, length us, event | category | flops | bytes accessed | tf_op | source)
XLA Modules:
  0.0 71.2 jit_solution(921834234281612304)
XLA Ops:
  0.0 1.5 %mix_levels.1 = f32[4,4,8,128]{3,2,1,0:T(8,128)} custom-call(bf16[2,8,1024]{2,1,0:T(8,128)(2,1)} %fields_ref.1, s32[8,1024]{1,0:T(8,128)} %bracket_ref.1, f32[8,1024]{1,0:T(8,128)} %fraction_ref.1), custom_call_target="tpu_custom_call" | custom-call | tf_op jit(solution)/shard_map/mix_levels/pallas_call | solution.py:152
  1.5 4.8 %all-to-all-start = ((f32[4,4,8,128]{3,2,1,0:T(8,128)}), f32[4,4,8,128]{3,2,1,0:T(8,128)S(1)}, u32[]{:S(2)}, u32[]{:S(2)}) async-start(f32[4,4,8,128]{3,2,1,0:T(8,128)} %mix_levels.1), calls=%async_computation | async-start | bytes 131072 | tf_op jit(solution)/shard_map/all_to_all | solution.py:157
  6.4 1.6 %count_entries.1.counts_ref = f32[56,128]{1,0:T(8,128)} custom-call(s32[3,32]{1,0:T(4,128)} %intersections_ref.1, s32[8,128]{1,0:T(8,128)} %bitcast.9), custom_call_target="tpu_custom_call" | custom-call | tf_op jit(solution)/shard_map/count_entries/pallas_call | solution.py:161
  8.0 2.8 %all-to-all-done.mixed_ref = f32[4,4,8,128]{3,2,1,0:T(8,128)S(1)} async-done(((f32[4,4,8,128]{3,2,1,0:T(8,128)}), f32[4,4,8,128]{3,2,1,0:T(8,128)S(1)}, u32[]{:S(2)}, u32[]{:S(2)}) %all-to-all-start) | async-done | bytes 65568 | tf_op jit(solution)/shard_map/all_to_all | solution.py:157
  10.8 0.0 copy-start
  10.8 0.6 copy-done
  11.5 2.1 %remap_blocks.1 = (f32[32,512]{1,0:T(8,128)}, f32[16,512]{1,0:T(8,128)}, f32[8,512]{1,0:T(8,128)}) custom-call(f32[4,4,8,128]{3,2,1,0:T(8,128)} %copy-done, bf16[16,128,128]{2,1,0:T(8,128)(2,1)} %weights_ref.1, f32[56,128]{1,0:T(8,128)} %count_entries.1.counts_ref), custom_call_target="tpu_custom_call" | custom-call | tf_op jit(solution)/shard_map/remap_blocks/pallas_call | solution.py:166
  13.6 13.6 %collective-permute-start = (f32[16,512]{1,0:T(8,128)}, f32[16,512]{1,0:T(8,128)S(1)}, u32[]{:S(2)}, u32[]{:S(2)}) collective-permute-start(f32[16,512]{1,0:T(8,128)} %get-tuple-element.11), channel_id=1, source_target_pairs={{0,504},{4,508},{8,16},{12,20},{16,8},{20,12},{24,32},{28,36},{32,... | collective-permute-start | bytes 98312 | tf_op jit(solution)/shard_map/ppermute | solution.py:182
  27.1 1.5 %collective-permute-done.cross_ref = f32[16,512]{1,0:T(8,128)S(1)} collective-permute-done((f32[16,512]{1,0:T(8,128)}, f32[16,512]{1,0:T(8,128)S(1)}, u32[]{:S(2)}, u32[]{:S(2)}) %collective-permute-start) | collective-permute-done | bytes 32800 | tf_op jit(solution)/shard_map/ppermute | solution.py:182
  28.6 0.0 copy-start.2
  28.6 0.6 copy-done.2
  29.2 1.5 %join_forwarded.1 = f32[32,512]{1,0:T(8,128)} custom-call(f32[32,512]{1,0:T(8,128)} %get-tuple-element.10.group_ref, f32[16,512]{1,0:T(8,128)} %copy-done.2), custom_call_target="tpu_custom_call" | custom-call | tf_op jit(solution)/shard_map/join_forwarded/pallas_call | solution.py:183
  30.7 6.4 %all-to-all-start.1 = ((f32[4,8,512]{2,1,0:T(8,128)}), f32[4,8,512]{2,1,0:T(8,128)S(1)}, u32[]{:S(2)}, u32[]{:S(2)}) async-start(f32[4,8,512]{2,1,0:T(8,128)} %bitcast.8), calls=%async_computation.1 | async-start | bytes 131072 | tf_op jit(solution)/shard_map/all_to_all | solution.py:188
  37.1 0.0 copy-done.5
  37.1 4.4 %collective-permute-start.1 = (f32[8,512]{1,0:T(8,128)S(1)}, f32[8,512]{1,0:T(8,128)S(1)}, u32[]{:S(2)}, u32[]{:S(2)}) collective-permute-start(f32[8,512]{1,0:T(8,128)S(1)} %copy-done.5), channel_id=1, source_target_pairs={{0,256},{4,260},{8,264},{12,268},{16,272},{20,276},{24,280},{28,28... | collective-permute-start | bytes 49160 | tf_op jit(solution)/shard_map/ppermute | solution.py:181
  41.5 3.9 %collective-permute-done.1.far_ref = f32[8,512]{1,0:T(8,128)S(1)} collective-permute-done((f32[8,512]{1,0:T(8,128)S(1)}, f32[8,512]{1,0:T(8,128)S(1)}, u32[]{:S(2)}, u32[]{:S(2)}) %collective-permute-start.1) | collective-permute-done | bytes 16416 | tf_op jit(solution)/shard_map/ppermute | solution.py:181
  45.5 0.0 all-to-all-done.1
  45.5 0.6 copy-done.3
  46.1 0.0 copy-done.1
  46.1 1.8 %filter_tiles.1 = (f32[4,8,128]{2,1,0:T(8,128)}, f32[128,1,128]{2,1,0:T(1,128)}) custom-call(f32[32,512]{1,0:T(8,128)} %bitcast.7, f32[8,512]{1,0:T(8,128)} %copy-done.3), custom_call_target="tpu_custom_call" | custom-call | tf_op jit(solution)/shard_map/filter_tiles/pallas_call | solution.py:190
  47.9 21.9 %all_to_all.21 = f32[128,1,128]{2,1,0:T(1,128)S(1)} all-to-all(f32[128,1,128]{2,1,0:T(1,128)} %get-tuple-element.14), channel_id=1, replica_groups=mesh['col'=128,'lev'=4] {'col'}, dimensions={0} | all-to-all | bytes 131072 | tf_op jit(solution)/shard_map/all_to_all | solution.py:198
  69.8 0.1 fusion.1
  69.9 0.6 copy-done.4
  70.5 0.7 subtract_multiply_fusion
  (7 shorter events, 0.1 us)
Async XLA Ops:
  1.5 9.3 %all-to-all-start = ((f32[4,4,8,128]{3,2,1,0:T(8,128)}), f32[4,4,8,128]{3,2,1,0:T(8,128)S(1)}, u32[]{:S(2)}, u32[]{:S(2)}) async-start(f32[4,4,8,128]{3,2,1,0:T(8,128)} %mix_levels.1), calls=%async_computation | async-start | bytes 131072 | tf_op jit(solution)/shard_map/all_to_all | solution.py:157
  10.8 0.6 copy-start
  13.6 15.1 %collective-permute-start = (f32[16,512]{1,0:T(8,128)}, f32[16,512]{1,0:T(8,128)S(1)}, u32[]{:S(2)}, u32[]{:S(2)}) collective-permute-start(f32[16,512]{1,0:T(8,128)} %get-tuple-element.11), channel_id=1, source_target_pairs={{0,504},{4,508},{8,16},{12,20},{16,8},{20,12},{24,32},{28,36},{32,... | collective-permute-start | bytes 98312 | tf_op jit(solution)/shard_map/ppermute | solution.py:182
  28.6 0.6 copy-start.2
  30.7 6.4 %copy-start.5 = (f32[8,512]{1,0:T(8,128)S(1)}, f32[8,512]{1,0:T(8,128)}, u32[]{:S(2)}) copy-start(f32[8,512]{1,0:T(8,128)} %get-tuple-element.12) | copy-start | bytes 49156
  30.7 14.7 %all-to-all-start.1 = ((f32[4,8,512]{2,1,0:T(8,128)}), f32[4,8,512]{2,1,0:T(8,128)S(1)}, u32[]{:S(2)}, u32[]{:S(2)}) async-start(f32[4,8,512]{2,1,0:T(8,128)} %bitcast.8), calls=%async_computation.1 | async-start | bytes 131072 | tf_op jit(solution)/shard_map/all_to_all | solution.py:188
  37.1 8.4 %collective-permute-start.1 = (f32[8,512]{1,0:T(8,128)S(1)}, f32[8,512]{1,0:T(8,128)S(1)}, u32[]{:S(2)}, u32[]{:S(2)}) collective-permute-start(f32[8,512]{1,0:T(8,128)S(1)} %copy-done.5), channel_id=1, source_target_pairs={{0,256},{4,260},{8,264},{12,268},{16,272},{20,276},{24,280},{28,28... | collective-permute-start | bytes 49160 | tf_op jit(solution)/shard_map/ppermute | solution.py:181
  45.5 0.6 copy-start.3
  45.5 0.6 copy-start.1
  69.8 0.7 %copy-start.4 = (f32[4,8,128]{2,1,0:T(8,128)S(1)}, f32[4,8,128]{2,1,0:T(8,128)}, u32[]{:S(2)}) copy-start(f32[4,8,128]{2,1,0:T(8,128)} %get-tuple-element.13) | copy-start | bytes 49156

commit v2 on v1

--- a/solution.py
+++ b/solution.py
@@ -5,6 +5,7 @@
 from jax.experimental.pallas import tpu as pltpu
 from jax.sharding import PartitionSpec as P
 
+
 F = 2
 PLEV = 8
 GROUP = 4
@@ -12,8 +13,10 @@
 
 epsilon = 1e-06
 
-
-def mix_kernel(fields_ref, bracket_ref, fraction_ref, out_ref):
+PARAMS = pltpu.CompilerParams(vmem_limit_bytes=4 << 20)
+
+
+def mix_levels(fields_ref, bracket_ref, fraction_ref, out_ref):
     levels = fields_ref.shape[1]
     lev_dev, rows, blocks, cols = out_ref.shape
     plev_dev = rows // F
@@ -33,7 +36,7 @@
                 ]
 
 
-def count_kernel(intersections_ref, owner_ref, out_ref):
+def count_entries(intersections_ref, owner_ref, out_ref):
     rows, pairs = out_ref.shape
     entries = intersections_ref.shape[1]
     tile_rows, lanes = owner_ref.shape
@@ -78,6 +81,45 @@
     )
 
 
+def prepare_kernel(
+    fields_hbm,
+    bracket_hbm,
+    fraction_hbm,
+    intersections_hbm,
+    owner_hbm,
+    weights_hbm,
+    mixed_ref,
+    counts_ref,
+    weights_ref,
+    fields_ref,
+    bracket_ref,
+    fraction_ref,
+    intersections_ref,
+    owner_ref,
+    sems,
+):
+    loads = [
+        pltpu.make_async_copy(source, target, sems.at[i])
+        for i, (source, target) in enumerate(
+            (
+                (fields_hbm, fields_ref),
+                (bracket_hbm, bracket_ref),
+                (fraction_hbm, fraction_ref),
+                (intersections_hbm, intersections_ref),
+                (owner_hbm, owner_ref),
+                (weights_hbm, weights_ref),
+            )
+        )
+    ]
+    for load in loads:
+        load.start()
+    for load in loads[:5]:
+        load.wait()
+    count_entries(intersections_ref, owner_ref, counts_ref)
+    mix_levels(fields_ref, bracket_ref, fraction_ref, mixed_ref)
+    loads[5].wait()
+
+
 def remap_kernel(mixed_ref, weights_ref, counts_ref, group_ref, cross_ref, far_ref, parts_ref):
     lev_dev, rows, blocks, cols = mixed_ref.shape
     cells = weights_ref.shape[2]
@@ -109,14 +151,6 @@
     far_ref[...] = total[n_group + n_cross :]
 
 
-def join_kernel(group_ref, cross_ref, out_ref):
-    half = cross_ref.shape[0]
-    upper = (lax.axis_index("col") % GROUP) >= CROSS
-    cross = cross_ref[...]
-    out_ref[:half] = group_ref[:half] + jnp.where(upper, 0.0, cross)
-    out_ref[half:] = group_ref[half:] + jnp.where(upper, cross, 0.0)
-
-
 def filter_kernel(near_ref, far_ref, filtered_ref, stats_ref):
     tile_dev = far_ref.shape[0]
     rows = filtered_ref.shape[0]
@@ -139,7 +173,7 @@
     stats_ref[...] = jnp.broadcast_to(stats[None], stats_ref.shape)
 
 
-def per_device(fields, bracket, fraction, remap_weights, intersections, tile_owner):
+def remap_step(fields, bracket, fraction, remap_weights, intersections, tile_owner):
     lev_dev = lax.axis_size("lev")
     col_count = lax.axis_size("col")
     plev_dev = PLEV // lev_dev
@@ -149,20 +183,32 @@
     rows = F * plev_dev
     f32 = jnp.float32
 
-    mixed = pl.pallas_call(
-        mix_kernel,
-        out_shape=jax.ShapeDtypeStruct((lev_dev, rows, blocks, block_cols), f32),
-        name="mix_levels",
-    )(fields, bracket, fraction)
-    mixed = lax.all_to_all(mixed, "lev", 0, 0, tiled=True)
-
     n_group = GROUP * tile_dev
     n_cross = CROSS * tile_dev
-    counts = pl.pallas_call(
-        count_kernel,
-        out_shape=jax.ShapeDtypeStruct((n_group + n_cross + tile_dev, weights_dev * blocks), f32),
-        name="count_entries",
-    )(intersections, tile_owner.reshape(-1, 128))
+    owner = tile_owner.reshape(-1, 128)
+    sources = (fields, bracket, fraction, intersections, owner, remap_weights)
+    anywhere = pl.BlockSpec(memory_space=pltpu.HBM)
+    mixed, counts, weights = pl.pallas_call(
+        prepare_kernel,
+        in_specs=[anywhere] * 6,
+        out_shape=[
+            jax.ShapeDtypeStruct((lev_dev, rows, blocks, block_cols), f32),
+            jax.ShapeDtypeStruct((n_group + n_cross + tile_dev, weights_dev * blocks), f32),
+            jax.ShapeDtypeStruct(remap_weights.shape, remap_weights.dtype),
+        ],
+        scratch_shapes=[
+            pltpu.VMEM(fields.shape, fields.dtype),
+            pltpu.VMEM(bracket.shape, bracket.dtype),
+            pltpu.VMEM(fraction.shape, fraction.dtype),
+            pltpu.VMEM(intersections.shape, intersections.dtype),
+            pltpu.VMEM(owner.shape, owner.dtype),
+            pltpu.SemaphoreType.DMA((6,)),
+        ],
+        name="mix_and_count",
+        compiler_params=PARAMS,
+    )(*[pltpu.with_memory_space_constraint(x, pltpu.HBM) for x in sources])
+    mixed = lax.all_to_all(mixed, "lev", 0, 0, tiled=True)
+
     group, cross, far = pl.pallas_call(
         remap_kernel,
         out_shape=[
@@ -170,7 +216,8 @@
         ],
         scratch_shapes=[pltpu.VMEM((weights_dev * blocks, rows * tile_cells), f32)],
         name="remap_blocks",
-    )(mixed, remap_weights, counts)
+        compiler_params=PARAMS,
+    )(mixed, weights, counts)
 
     swap = [
         (d, (d - CROSS) % col_count if d % GROUP < CROSS else (d + CROSS) % col_count)
@@ -180,11 +227,8 @@
     groups = [[g * GROUP + k for k in range(GROUP)] for g in range(col_count // GROUP)]
     far = lax.ppermute(far, "col", opposite)
     cross = lax.ppermute(cross, "col", swap)
-    near = pl.pallas_call(
-        join_kernel,
-        out_shape=jax.ShapeDtypeStruct((n_group, rows * tile_cells), f32),
-        name="join_forwarded",
-    )(group, cross)
+    upper = lax.axis_index("col") % GROUP >= CROSS
+    near = group + jnp.concatenate([jnp.where(upper, 0.0, cross), jnp.where(upper, cross, 0.0)])
     near = lax.all_to_all(near, "col", 0, 0, tiled=True, axis_index_groups=groups)
 
     filtered, stats = pl.pallas_call(
@@ -194,6 +238,7 @@
             jax.ShapeDtypeStruct((col_count, 1, tile_cells), f32),
         ],
         name="filter_tiles",
+        compiler_params=PARAMS,
     )(near, far)
     stats = lax.all_to_all(stats, "col", 0, 0, tiled=True)[:, 0]
     count = float(tile_dev * tile_cells)
@@ -217,5 +262,5 @@
     )
     out_specs = P(None, "lev", "col", None)
     return jax.shard_map(
-        per_device, mesh=mesh, in_specs=in_specs, out_specs=out_specs, check_vma=False
-    )
+        remap_step, mesh=mesh, in_specs=in_specs, out_specs=out_specs, check_vma=False
+    )

time: 71.9 us -> 64 us (0.89)
  blocking collectives: 21.9 us -> 30.8 us
  Pallas kernels: 8.5 us -> 1.91 us
  starting transfers between devices: 29.2 us -> 24.2 us
  waiting for transfers between devices: 8.3 us -> 5.23 us
  local copies, waits for them, and re-layouts: 2.48 us -> 0 us
    all_to_all x1 -> x2, blocking collectives: 21.9 us -> 30.8 us  [the longest x1 21.7 us: remap_step(): stats = lax.all_to_all(stats, 'col', 0, 0, tiled=True)[:, 0]]
    pallas_call x5 -> x3, Pallas kernels: 8.5 us -> 1.91 us  [the longest x1 1.2 us: remap_step(): pl.pallas_call(prepare_kernel, in_specs=[anywhere] * 6, out_shape=[jax.Sh...]
    all_to_all x2 -> x1, starting transfers between devices: 11.2 us -> 6.22 us  [remap_step(): lax.all_to_all(near, 'col', 0, 0, tiled=True, axis_index_groups=groups)]
    all_to_all x2 -> x1, waiting for transfers between devices: 2.85 us -> 0.01 us  [remap_step(): lax.all_to_all(near, 'col', 0, 0, tiled=True, axis_index_groups=groups)]
    unnamed x12 -> x0, local copies, waits for them, and re-layouts: 2.48 us -> none
  transfers between devices with their start and end apart: 4 -> 3, of which waited for: 3 -> 2; matrix products, arithmetic and copies ran while one was open for 0% -> 0% of each run, Pallas kernels for 2% -> 0%
where the time goes in v2:
time: 64 us; the launch traced here: 63.7 us
  blocking collectives  30.8 us (48%)
  starting transfers between devices  24.2 us (38%)
  waiting for transfers between devices  5.23 us (8%)
  Pallas kernels  1.91 us (3%)
  other arithmetic  1.48 us (2%)
    all_to_all x1, blocking collectives, remap_step(): stats = lax.all_to_all(stats, 'col', 0, 0, tiled=True)[:, 0]  21.7 us
    ppermute x1, starting transfers between devices, remap_step(): cross = lax.ppermute(cross, 'col', swap)  13.6 us
    all_to_all x1, blocking collectives, remap_step(): mixed = lax.all_to_all(mixed, 'lev', 0, 0, tiled=True)  9.11 us
    all_to_all x1, starting transfers between devices, remap_step(): lax.all_to_all(near, 'col', 0, 0, tiled=True, axis_index_groups=groups)  6.22 us
    ppermute x1, starting transfers between devices, remap_step(): far = lax.ppermute(far, 'col', opposite)  4.42 us
    ppermute x1, waiting for transfers between devices, remap_step(): far = lax.ppermute(far, 'col', opposite)  3.95 us
  transfers between devices with their start and end apart: 3, of which 2 were waited for; matrix products, arithmetic and copies ran while one was open for 0% of the time, Pallas kernels for 0%

profile of v2, /device:TPU:1, one launch (start us, length us, event | category | flops | bytes accessed | tf_op | source)
XLA Modules:
  0.0 63.7 jit_solution(12191996665739445244)
XLA Ops:
  0.0 1.2 %mix_and_count.1 = (f32[4,4,8,128]{3,2,1,0:T(8,128)S(1)}, f32[56,128]{1,0:T(8,128)S(1)}, bf16[16,128,128]{2,1,0:T(8,128)(2,1)S(1)}) custom-call(bf16[2,8,1024]{2,1,0:T(8,128)(2,1)} %fields_hbm.1, s32[8,1024]{1,0:T(8,128)} %bracket_hbm.1, f32[8,1024]{1,0:T(8,128)} %fraction_hbm.1, s32[3,32]{1,0:T(4,128)} %intersections_hbm.1, s32[8,128]{1,0:T(8,128)} %bitcast.9, ...), custom_call_target="tpu_custom_call" | custom-call | tf_op jit(solution)/shard_map/mix_and_count/pallas_call | solution.py:191
  1.2 9.1 %all_to_all.21.mixed_ref = f32[4,4,8,128]{3,2,1,0:T(8,128)S(1)} all-to-all(f32[4,4,8,128]{3,2,1,0:T(8,128)S(1)} %get-tuple-element.13), channel_id=1, replica_groups=mesh['col'=128,'lev'=4] {'lev'}, dimensions={0} | all-to-all | bytes 131072 | tf_op jit(solution)/shard_map/all_to_all | solution.py:210
  10.3 0.4 remap_blocks.1
  10.8 13.6 %collective-permute-start = (f32[16,512]{1,0:T(8,128)S(1)}, f32[16,512]{1,0:T(8,128)S(1)}, u32[]{:S(2)}, u32[]{:S(2)}) collective-permute-start(f32[16,512]{1,0:T(8,128)S(1)} %get-tuple-element.17), channel_id=1, source_target_pairs={{0,504},{4,508},{8,16},{12,20},{16,8},{20,12},{24,32},{28,36},{32,... | collective-permute-start | bytes 98312 | tf_op jit(solution)/shard_map/ppermute | solution.py:229
  24.3 1.3 %collective-permute-done = f32[16,512]{1,0:T(8,128)S(1)} collective-permute-done((f32[16,512]{1,0:T(8,128)S(1)}, f32[16,512]{1,0:T(8,128)S(1)}, u32[]{:S(2)}, u32[]{:S(2)}) %collective-permute-start) | collective-permute-done | bytes 32800 | tf_op jit(solution)/shard_map/ppermute | solution.py:229
  25.6 0.6 fusion.2
  26.3 6.2 %all-to-all-start.1 = ((f32[4,8,512]{2,1,0:T(8,128)}), f32[4,8,512]{2,1,0:T(8,128)S(1)}, u32[]{:S(2)}, u32[]{:S(2)}) async-start(f32[4,8,512]{2,1,0:T(8,128)} %fusion.2), calls=%async_computation.1 | async-start | bytes 131072 | tf_op jit(solution)/shard_map/all_to_all | solution.py:232
  32.5 4.4 %collective-permute-start.1 = (f32[8,512]{1,0:T(8,128)S(1)}, f32[8,512]{1,0:T(8,128)S(1)}, u32[]{:S(2)}, u32[]{:S(2)}) collective-permute-start(f32[8,512]{1,0:T(8,128)S(1)} %get-tuple-element.18), channel_id=1, source_target_pairs={{0,256},{4,260},{8,264},{12,268},{16,272},{20,276},{24,280},{28,28... | collective-permute-start | bytes 49160 | tf_op jit(solution)/shard_map/ppermute | solution.py:228
  36.9 3.9 %collective-permute-done.1.far_ref = f32[8,512]{1,0:T(8,128)S(1)} collective-permute-done((f32[8,512]{1,0:T(8,128)S(1)}, f32[8,512]{1,0:T(8,128)S(1)}, u32[]{:S(2)}, u32[]{:S(2)}) %collective-permute-start.1) | collective-permute-done | bytes 16416 | tf_op jit(solution)/shard_map/ppermute | solution.py:228
  40.9 0.0 all-to-all-done.1
  40.9 0.3 filter_tiles.1
  41.2 21.7 %all_to_all.22 = f32[128,1,128]{2,1,0:T(1,128)S(1)} all-to-all(f32[128,1,128]{2,1,0:T(1,128)S(1)} %get-tuple-element.20), channel_id=1, replica_groups=mesh['col'=128,'lev'=4] {'col'}, dimensions={0} | all-to-all | bytes 131072 | tf_op jit(solution)/shard_map/all_to_all | solution.py:243
  62.9 0.1 fusion.1
  63.0 0.7 %subtract_multiply_fusion = f32[4,8,128]{2,1,0:T(8,128)} fusion(f32[4,8,128]{2,1,0:T(8,128)S(1)} %get-tuple-element.19, f32[4]{0:T(128)S(1)} %add_rsqrt_fusion, f32[4]{0:T(128)S(1)} %broadcast_multiply_fusion), kind=kLoop, calls=%fused_computation.6 | loop fusion | flops 8192 | bytes 32800 | tf_op jit(solution)/shard_map/mul | solution.py:250
  (4 shorter events, 0.1 us)
Async XLA Ops:
  10.8 14.9 %collective-permute-start = (f32[16,512]{1,0:T(8,128)S(1)}, f32[16,512]{1,0:T(8,128)S(1)}, u32[]{:S(2)}, u32[]{:S(2)}) collective-permute-start(f32[16,512]{1,0:T(8,128)S(1)} %get-tuple-element.17), channel_id=1, source_target_pairs={{0,504},{4,508},{8,16},{12,20},{16,8},{20,12},{24,32},{28,36},{32,... | collective-permute-start | bytes 98312 | tf_op jit(solution)/shard_map/ppermute | solution.py:229
  26.3 14.6 %all-to-all-start.1 = ((f32[4,8,512]{2,1,0:T(8,128)}), f32[4,8,512]{2,1,0:T(8,128)S(1)}, u32[]{:S(2)}, u32[]{:S(2)}) async-start(f32[4,8,512]{2,1,0:T(8,128)} %fusion.2), calls=%async_computation.1 | async-start | bytes 131072 | tf_op jit(solution)/shard_map/all_to_all | solution.py:232
  32.5 8.4 %collective-permute-start.1 = (f32[8,512]{1,0:T(8,128)S(1)}, f32[8,512]{1,0:T(8,128)S(1)}, u32[]{:S(2)}, u32[]{:S(2)}) collective-permute-start(f32[8,512]{1,0:T(8,128)S(1)} %get-tuple-element.18), channel_id=1, source_target_pairs={{0,256},{4,260},{8,264},{12,268},{16,272},{20,276},{24,280},{28,28... | collective-permute-start | bytes 49160 | tf_op jit(solution)/shard_map/ppermute | solution.py:228

commit v3 on v2

--- a/solution.py
+++ b/solution.py
@@ -10,6 +10,8 @@
 PLEV = 8
 GROUP = 4
 CROSS = 2
+ROW = 16
+EARLY = 2
 
 epsilon = 1e-06
 
@@ -151,11 +153,11 @@
     far_ref[...] = total[n_group + n_cross :]
 
 
-def filter_kernel(near_ref, far_ref, filtered_ref, stats_ref):
+def filter_kernel(near_ref, far_ref, late_ref, filtered_ref, stats_ref):
     tile_dev = far_ref.shape[0]
     rows = filtered_ref.shape[0]
     cells = filtered_ref.shape[2]
-    total = far_ref[...]
+    total = far_ref[...] + late_ref[...]
     for k in range(near_ref.shape[0] // tile_dev):
         total = total + near_ref[k * tile_dev : (k + 1) * tile_dev]
     lane = lax.broadcasted_iota(jnp.int32, (1, cells), 1)
@@ -224,8 +226,11 @@
         for d in range(col_count)
     ]
     opposite = [(d, (d + col_count // 2) % col_count) for d in range(col_count)]
+    early = [pair for pair in opposite if pair[0] % ROW < EARLY]
+    late = [pair for pair in opposite if pair[0] % ROW >= EARLY]
     groups = [[g * GROUP + k for k in range(GROUP)] for g in range(col_count // GROUP)]
-    far = lax.ppermute(far, "col", opposite)
+    far_a = lax.ppermute(far, "col", early)
+    far_b = lax.ppermute(far, "col", late)
     cross = lax.ppermute(cross, "col", swap)
     upper = lax.axis_index("col") % GROUP >= CROSS
     near = group + jnp.concatenate([jnp.where(upper, 0.0, cross), jnp.where(upper, cross, 0.0)])
@@ -239,8 +244,10 @@
         ],
         name="filter_tiles",
         compiler_params=PARAMS,
-    )(near, far)
-    stats = lax.all_to_all(stats, "col", 0, 0, tiled=True)[:, 0]
+    )(near, far_a, far_b)
+    lead = 72
+    order = [(lead + k) % col_count for k in range(col_count)]
+    stats = lax.all_to_all(stats, "col", 0, 0, tiled=True, axis_index_groups=[order])[:, 0]
     count = float(tile_dev * tile_cells)
     field_mean = jnp.sum(stats[:, :rows], axis=0) / float(col_count)
     apart = stats[:, :rows] - field_mean[None]

time: 64 us -> 60.2 us (0.941)
  blocking collectives: 30.8 us -> 26.9 us
  starting transfers between devices: 24.2 us -> 24.9 us
  waiting for transfers between devices: 5.23 us -> 4.56 us
    all_to_all x1, blocking collectives: 21.7 us -> 17.8 us  [remap_step(): lax.all_to_all(stats, 'col', 0, 0, tiled=True, axis_index_groups=[order])]
    ppermute x1 -> x2, waiting for transfers between devices: 3.95 us -> 3.28 us  [the longest x1 3.28 us: remap_step(): far_a = lax.ppermute(far, 'col', early)]
    ppermute x1 -> x2, starting transfers between devices: 4.42 us -> 5.08 us  [the longest x1 4.42 us: remap_step(): far_a = lax.ppermute(far, 'col', early)]
  transfers between devices with their start and end apart: 3 -> 4, of which waited for: 2 -> 2; matrix products, arithmetic and copies ran while one was open for 0% -> 0% of each run, Pallas kernels for 0% -> 0%
where the time goes in v3:
time: 60.2 us; the launch traced here: 59.8 us
  blocking collectives  26.9 us (45%)
  starting transfers between devices  24.9 us (41%)
  waiting for transfers between devices  4.56 us (8%)
  Pallas kernels  1.91 us (3%)
  other arithmetic  1.48 us (2%)
    all_to_all x1, blocking collectives, remap_step(): lax.all_to_all(stats, 'col', 0, 0, tiled=True, axis_index_groups=[order])  17.8 us
    ppermute x1, starting transfers between devices, remap_step(): cross = lax.ppermute(cross, 'col', swap)  13.6 us
    all_to_all x1, blocking collectives, remap_step(): mixed = lax.all_to_all(mixed, 'lev', 0, 0, tiled=True)  9.11 us
    all_to_all x1, starting transfers between devices, remap_step(): lax.all_to_all(near, 'col', 0, 0, tiled=True, axis_index_groups=groups)  6.22 us
    ppermute x1, starting transfers between devices, remap_step(): far_a = lax.ppermute(far, 'col', early)  4.42 us
    ppermute x1, waiting for transfers between devices, remap_step(): far_a = lax.ppermute(far, 'col', early)  3.28 us
    ppermute x1, waiting for transfers between devices, remap_step(): cross = lax.ppermute(cross, 'col', swap)  1.28 us
  transfers between devices with their start and end apart: 4, of which 2 were waited for; matrix products, arithmetic and copies ran while one was open for 0% of the time, Pallas kernels for 0%

profile of v3, /device:TPU:1, one launch (start us, length us, event | category | flops | bytes accessed | tf_op | source)
XLA Modules:
  0.0 59.8 jit_solution(4518051223007626717)
XLA Ops:
  0.0 1.2 %mix_and_count.1 = (f32[4,4,8,128]{3,2,1,0:T(8,128)S(1)}, f32[56,128]{1,0:T(8,128)S(1)}, bf16[16,128,128]{2,1,0:T(8,128)(2,1)S(1)}) custom-call(bf16[2,8,1024]{2,1,0:T(8,128)(2,1)} %fields_hbm.1, s32[8,1024]{1,0:T(8,128)} %bracket_hbm.1, f32[8,1024]{1,0:T(8,128)} %fraction_hbm.1, s32[3,32]{1,0:T(4,128)} %intersections_hbm.1, s32[8,128]{1,0:T(8,128)} %bitcast.9, ...), custom_call_target="tpu_custom_call" | custom-call | tf_op jit(solution)/shard_map/mix_and_count/pallas_call | solution.py:193
  1.2 9.1 %all_to_all.21.mixed_ref = f32[4,4,8,128]{3,2,1,0:T(8,128)S(1)} all-to-all(f32[4,4,8,128]{3,2,1,0:T(8,128)S(1)} %get-tuple-element.13), channel_id=1, replica_groups=mesh['col'=128,'lev'=4] {'lev'}, dimensions={0} | all-to-all | bytes 131072 | tf_op jit(solution)/shard_map/all_to_all | solution.py:212
  10.3 0.4 remap_blocks.1
  10.8 13.6 %collective-permute-start = (f32[16,512]{1,0:T(8,128)S(1)}, f32[16,512]{1,0:T(8,128)S(1)}, u32[]{:S(2)}, u32[]{:S(2)}) collective-permute-start(f32[16,512]{1,0:T(8,128)S(1)} %get-tuple-element.17), channel_id=1, source_target_pairs={{0,504},{4,508},{8,16},{12,20},{16,8},{20,12},{24,32},{28,36},{32,... | collective-permute-start | bytes 98312 | tf_op jit(solution)/shard_map/ppermute | solution.py:234
  24.3 1.3 %collective-permute-done = f32[16,512]{1,0:T(8,128)S(1)} collective-permute-done((f32[16,512]{1,0:T(8,128)S(1)}, f32[16,512]{1,0:T(8,128)S(1)}, u32[]{:S(2)}, u32[]{:S(2)}) %collective-permute-start) | collective-permute-done | bytes 32800 | tf_op jit(solution)/shard_map/ppermute | solution.py:234
  25.6 0.6 %fusion.2 = f32[4,8,512]{2,1,0:T(8,128)} fusion(f32[32,512]{1,0:T(8,128)S(1)} %get-tuple-element.16, f32[16,512]{1,0:T(8,128)S(1)} %get-tuple-element.22, f32[16,512]{1,0:T(8,128)S(1)} %get-tuple-element.21), kind=kLoop, calls=%fused_computation.4 | loop fusion | flops 32768 | bytes 196608 | tf_op jit(solution)/shard_map/all_to_all | solution.py:237
  26.3 6.2 %all-to-all-start.1 = ((f32[4,8,512]{2,1,0:T(8,128)}), f32[4,8,512]{2,1,0:T(8,128)S(1)}, u32[]{:S(2)}, u32[]{:S(2)}) async-start(f32[4,8,512]{2,1,0:T(8,128)} %fusion.2), calls=%async_computation.1 | async-start | bytes 131072 | tf_op jit(solution)/shard_map/all_to_all | solution.py:237
  32.5 4.4 %collective-permute-start.1 = (f32[8,512]{1,0:T(8,128)S(1)}, f32[8,512]{1,0:T(8,128)S(1)}, u32[]{:S(2)}, u32[]{:S(2)}) collective-permute-start(f32[8,512]{1,0:T(8,128)S(1)} %get-tuple-element.18), channel_id=1, source_target_pairs={{0,256},{4,260},{64,320},{68,324},{128,384},{132,388},{192,448},{1... | collective-permute-start | bytes 49160 | tf_op jit(solution)/shard_map/ppermute | solution.py:232
  36.9 0.7 %collective-permute-start.2 = (f32[8,512]{1,0:T(8,128)S(1)}, f32[8,512]{1,0:T(8,128)S(1)}, u32[]{:S(2)}, u32[]{:S(2)}) collective-permute-start(f32[8,512]{1,0:T(8,128)S(1)} %get-tuple-element.18), channel_id=1, source_target_pairs={{8,264},{12,268},{16,272},{20,276},{24,280},{28,284},{32,288},{36,... | collective-permute-start | bytes 49160 | tf_op jit(solution)/shard_map/ppermute | solution.py:233
  37.6 3.3 %collective-permute-done.1.far_ref = f32[8,512]{1,0:T(8,128)S(1)} collective-permute-done((f32[8,512]{1,0:T(8,128)S(1)}, f32[8,512]{1,0:T(8,128)S(1)}, u32[]{:S(2)}, u32[]{:S(2)}) %collective-permute-start.1) | collective-permute-done | bytes 16416 | tf_op jit(solution)/shard_map/ppermute | solution.py:232
  40.9 0.0 collective-permute-done.2.late_ref
  40.9 0.0 all-to-all-done.1
  40.9 0.3 filter_tiles.1
  41.2 17.8 %all_to_all.22 = f32[128,1,128]{2,1,0:T(1,128)S(1)} all-to-all(f32[128,1,128]{2,1,0:T(1,128)S(1)} %get-tuple-element.20), channel_id=1, replica_groups={{288,292,296,300,304,308,312,316,320,324,328,332,336,340,344,348,352,35..., dimensions={0} | all-to-all | bytes 131072 | tf_op jit(solution)/shard_map/all_to_all | solution.py:250
  59.0 0.1 fusion.1
  59.1 0.7 %subtract_multiply_fusion = f32[4,8,128]{2,1,0:T(8,128)} fusion(f32[4,8,128]{2,1,0:T(8,128)S(1)} %get-tuple-element.19, f32[4]{0:T(128)S(1)} %add_rsqrt_fusion, f32[4]{0:T(128)S(1)} %broadcast_multiply_fusion), kind=kLoop, calls=%fused_computation.6 | loop fusion | flops 8192 | bytes 32800 | tf_op jit(solution)/shard_map/mul | solution.py:257
  (4 shorter events, 0.1 us)
Async XLA Ops:
  10.8 14.9 %collective-permute-start = (f32[16,512]{1,0:T(8,128)S(1)}, f32[16,512]{1,0:T(8,128)S(1)}, u32[]{:S(2)}, u32[]{:S(2)}) collective-permute-start(f32[16,512]{1,0:T(8,128)S(1)} %get-tuple-element.17), channel_id=1, source_target_pairs={{0,504},{4,508},{8,16},{12,20},{16,8},{20,12},{24,32},{28,36},{32,... | collective-permute-start | bytes 98312 | tf_op jit(solution)/shard_map/ppermute | solution.py:234
  26.3 14.6 %all-to-all-start.1 = ((f32[4,8,512]{2,1,0:T(8,128)}), f32[4,8,512]{2,1,0:T(8,128)S(1)}, u32[]{:S(2)}, u32[]{:S(2)}) async-start(f32[4,8,512]{2,1,0:T(8,128)} %fusion.2), calls=%async_computation.1 | async-start | bytes 131072 | tf_op jit(solution)/shard_map/all_to_all | solution.py:237
  32.5 8.4 %collective-permute-start.1 = (f32[8,512]{1,0:T(8,128)S(1)}, f32[8,512]{1,0:T(8,128)S(1)}, u32[]{:S(2)}, u32[]{:S(2)}) collective-permute-start(f32[8,512]{1,0:T(8,128)S(1)} %get-tuple-element.18), channel_id=1, source_target_pairs={{0,256},{4,260},{64,320},{68,324},{128,384},{132,388},{192,448},{1... | collective-permute-start | bytes 49160 | tf_op jit(solution)/shard_map/ppermute | solution.py:232
  36.9 4.0 %collective-permute-start.2 = (f32[8,512]{1,0:T(8,128)S(1)}, f32[8,512]{1,0:T(8,128)S(1)}, u32[]{:S(2)}, u32[]{:S(2)}) collective-permute-start(f32[8,512]{1,0:T(8,128)S(1)} %get-tuple-element.18), channel_id=1, source_target_pairs={{8,264},{12,268},{16,272},{20,276},{24,280},{28,284},{32,288},{36,... | collective-permute-start | bytes 49160 | tf_op jit(solution)/shard_map/ppermute | solution.py:233

commit v4 on v3

--- a/solution.py
+++ b/solution.py
@@ -12,6 +12,9 @@
 CROSS = 2
 ROW = 16
 EARLY = 2
+LEV_FIRST = 2
+NEAR_FIRST = 3
+STATS_FIRST = 89
 
 epsilon = 1e-06
 
@@ -33,7 +36,7 @@
     for f in range(F):
         for p in range(lev_dev * plev_dev):
             for s in range(blocks):
-                out_ref[p // plev_dev, f * plev_dev + p % plev_dev, s : s + 1, :] = acc[f][
+                out_ref[(p // plev_dev - LEV_FIRST) % lev_dev, f * plev_dev + p % plev_dev, s : s + 1, :] = acc[f][
                     p : p + 1, s * cols : (s + 1) * cols
                 ]
 
@@ -71,7 +74,7 @@
     local = slot % tile_dev
     far = dev == (me + col_count // 2) % col_count
     same = dev // GROUP == me // GROUP
-    block = jnp.where(same, dev % GROUP, jnp.where(far, GROUP + CROSS, GROUP + dev % CROSS))
+    block = jnp.where(same, (dev + GROUP - NEAR_FIRST) % GROUP, jnp.where(far, GROUP + CROSS, GROUP + dev % CROSS))
     row = block * tile_dev + local
     rows_hit = lax.broadcasted_iota(jnp.int32, (rows, entries), 0) == row
     pair = weight * float(blocks) + source
@@ -153,6 +156,18 @@
     far_ref[...] = total[n_group + n_cross :]
 
 
+def join_kernel(group_ref, cross_ref, out_ref):
+    tile_dev = cross_ref.shape[0] // CROSS
+    upper = lax.axis_index("col") % GROUP >= CROSS
+    for i in range(GROUP):
+        member = (i + NEAR_FIRST) % GROUP
+        mine = upper if member >= CROSS else jnp.logical_not(upper)
+        start = member % CROSS * tile_dev
+        forwarded = cross_ref[start : start + tile_dev]
+        rows = slice(i * tile_dev, (i + 1) * tile_dev)
+        out_ref[rows] = group_ref[rows] + jnp.where(mine, forwarded, 0.0)
+
+
 def filter_kernel(near_ref, far_ref, late_ref, filtered_ref, stats_ref):
     tile_dev = far_ref.shape[0]
     rows = filtered_ref.shape[0]
@@ -209,7 +224,8 @@
         name="mix_and_count",
         compiler_params=PARAMS,
     )(*[pltpu.with_memory_space_constraint(x, pltpu.HBM) for x in sources])
-    mixed = lax.all_to_all(mixed, "lev", 0, 0, tiled=True)
+    levs = [[(k + LEV_FIRST) % lev_dev for k in range(lev_dev)]]
+    mixed = lax.all_to_all(mixed, "lev", 0, 0, tiled=True, axis_index_groups=levs)
 
     group, cross, far = pl.pallas_call(
         remap_kernel,
@@ -228,12 +244,16 @@
     opposite = [(d, (d + col_count // 2) % col_count) for d in range(col_count)]
     early = [pair for pair in opposite if pair[0] % ROW < EARLY]
     late = [pair for pair in opposite if pair[0] % ROW >= EARLY]
-    groups = [[g * GROUP + k for k in range(GROUP)] for g in range(col_count // GROUP)]
+    groups = [[g * GROUP + (k + NEAR_FIRST) % GROUP for k in range(GROUP)] for g in range(col_count // GROUP)]
     far_a = lax.ppermute(far, "col", early)
     far_b = lax.ppermute(far, "col", late)
     cross = lax.ppermute(cross, "col", swap)
-    upper = lax.axis_index("col") % GROUP >= CROSS
-    near = group + jnp.concatenate([jnp.where(upper, 0.0, cross), jnp.where(upper, cross, 0.0)])
+    near = pl.pallas_call(
+        join_kernel,
+        out_shape=jax.ShapeDtypeStruct((n_group, rows * tile_cells), f32),
+        name="join_forwarded",
+        compiler_params=PARAMS,
+    )(group, cross)
     near = lax.all_to_all(near, "col", 0, 0, tiled=True, axis_index_groups=groups)
 
     filtered, stats = pl.pallas_call(
@@ -245,8 +265,8 @@
         name="filter_tiles",
         compiler_params=PARAMS,
     )(near, far_a, far_b)
-    lead = 72
-    order = [(lead + k) % col_count for k in range(col_count)]
+    lead = STATS_FIRST
+    order = sorted(range(col_count), key=lambda d: (d != lead, d % ROW, d))
     stats = lax.all_to_all(stats, "col", 0, 0, tiled=True, axis_index_groups=[order])[:, 0]
     count = float(tile_dev * tile_cells)
     field_mean = jnp.sum(stats[:, :rows], axis=0) / float(col_count)

time: 60.2 us -> 57.7 us (0.958)
  blocking collectives: 26.9 us -> 24.8 us
  starting transfers between devices: 24.9 us -> 23.9 us
  waiting for transfers between devices: 4.56 us -> 5.23 us
  other arithmetic: 1.48 us -> 0.84 us
  Pallas kernels: 1.91 us -> 2.53 us
    all_to_all x1, blocking collectives: 9.11 us -> 7.62 us  [remap_step(): lax.all_to_all(mixed, 'lev', 0, 0, tiled=True, axis_index_groups=levs)]
    all_to_all x1, starting transfers between devices: 6.22 us -> 5.23 us  [remap_step(): lax.all_to_all(near, 'col', 0, 0, tiled=True, axis_index_groups=groups)]
    all_to_all x1, blocking collectives: 17.8 us -> 17.2 us  [remap_step(): lax.all_to_all(stats, 'col', 0, 0, tiled=True, axis_index_groups=[order])]
    ppermute x1, waiting for transfers between devices: 3.28 us -> 3.94 us  [remap_step(): far_a = lax.ppermute(far, 'col', early)]
    all_to_all x1 -> x0, other arithmetic: 0.63 us -> none  [remap_step(): lax.all_to_all(near, 'col', 0, 0, tiled=True, axis_index_groups=groups)]
    pallas_call x0 -> x1, Pallas kernels: none -> 0.62 us  [remap_step(): pl.pallas_call(join_kernel, out_shape=jax.ShapeDtypeStruct((n_group, rows...]
where the time goes in v4:
time: 57.7 us; the launch traced here: 57.3 us
  blocking collectives  24.8 us (43%)
  starting transfers between devices  23.9 us (41%)
  waiting for transfers between devices  5.23 us (9%)
  Pallas kernels  2.53 us (4%)
  other arithmetic  0.84 us (1%)
    all_to_all x1, blocking collectives, remap_step(): lax.all_to_all(stats, 'col', 0, 0, tiled=True, axis_index_groups=[order])  17.2 us
    ppermute x1, starting transfers between devices, remap_step(): cross = lax.ppermute(cross, 'col', swap)  13.6 us
    all_to_all x1, blocking collectives, remap_step(): lax.all_to_all(mixed, 'lev', 0, 0, tiled=True, axis_index_groups=levs)  7.62 us
    all_to_all x1, starting transfers between devices, remap_step(): lax.all_to_all(near, 'col', 0, 0, tiled=True, axis_index_groups=groups)  5.23 us
    ppermute x1, starting transfers between devices, remap_step(): far_a = lax.ppermute(far, 'col', early)  4.43 us
    ppermute x1, waiting for transfers between devices, remap_step(): far_a = lax.ppermute(far, 'col', early)  3.94 us
    ppermute x1, waiting for transfers between devices, remap_step(): cross = lax.ppermute(cross, 'col', swap)  1.29 us
    pallas_call x1, Pallas kernels, remap_step(): pl.pallas_call(prepare_kernel, in_specs=[anywhere] * 6, out_shape=[jax.Sh...  1.2 us
  transfers between devices with their start and end apart: 4, of which 2 were waited for; matrix products, arithmetic and copies ran while one was open for 0% of the time, Pallas kernels for 0%

profile of v4, /device:TPU:1, one launch (start us, length us, event | category | flops | bytes accessed | tf_op | source)
XLA Modules:
  0.0 57.3 jit_solution(7064454952206346794)
XLA Ops:
  0.0 1.2 %mix_and_count.1 = (f32[4,4,8,128]{3,2,1,0:T(8,128)S(1)}, f32[56,128]{1,0:T(8,128)S(1)}, bf16[16,128,128]{2,1,0:T(8,128)(2,1)S(1)}) custom-call(bf16[2,8,1024]{2,1,0:T(8,128)(2,1)} %fields_hbm.1, s32[8,1024]{1,0:T(8,128)} %bracket_hbm.1, f32[8,1024]{1,0:T(8,128)} %fraction_hbm.1, s32[3,32]{1,0:T(4,128)} %intersections_hbm.1, s32[8,128]{1,0:T(8,128)} %bitcast.8, ...), custom_call_target="tpu_custom_call" | custom-call | tf_op jit(solution)/shard_map/mix_and_count/pallas_call | solution.py:208
  1.2 7.6 %all_to_all.21.mixed_ref = f32[4,4,8,128]{3,2,1,0:T(8,128)S(1)} all-to-all(f32[4,4,8,128]{3,2,1,0:T(8,128)S(1)} %get-tuple-element.13), channel_id=1, replica_groups={{2,3,0,1},{6,7,4,5},{10,11,8,9},{14,15,12,13},{18,19,16,17},{22,23,20,2..., dimensions={0} | all-to-all | bytes 131072 | tf_op jit(solution)/shard_map/all_to_all | solution.py:228
  8.8 0.4 remap_blocks.1
  9.3 13.6 %collective-permute-start = (f32[16,512]{1,0:T(8,128)S(1)}, f32[16,512]{1,0:T(8,128)S(1)}, u32[]{:S(2)}, u32[]{:S(2)}) collective-permute-start(f32[16,512]{1,0:T(8,128)S(1)} %get-tuple-element.17), channel_id=1, source_target_pairs={{0,504},{4,508},{8,16},{12,20},{16,8},{20,12},{24,32},{28,36},{32,... | collective-permute-start | bytes 98312 | tf_op jit(solution)/shard_map/ppermute | solution.py:250
  22.8 1.3 %collective-permute-done.cross_ref = f32[16,512]{1,0:T(8,128)S(1)} collective-permute-done((f32[16,512]{1,0:T(8,128)S(1)}, f32[16,512]{1,0:T(8,128)S(1)}, u32[]{:S(2)}, u32[]{:S(2)}) %collective-permute-start) | collective-permute-done | bytes 32800 | tf_op jit(solution)/shard_map/ppermute | solution.py:250
  24.1 0.6 %join_forwarded.1 = f32[32,512]{1,0:T(8,128)} custom-call(f32[32,512]{1,0:T(8,128)S(1)} %get-tuple-element.16.group_ref, f32[16,512]{1,0:T(8,128)S(1)} %collective-permute-done.cross_ref), custom_call_target="tpu_custom_call" | custom-call | tf_op jit(solution)/shard_map/join_forwarded/pallas_call | solution.py:251
  24.8 5.2 %all-to-all-start.1 = ((f32[4,8,512]{2,1,0:T(8,128)}), f32[4,8,512]{2,1,0:T(8,128)S(1)}, u32[]{:S(2)}, u32[]{:S(2)}) async-start(f32[4,8,512]{2,1,0:T(8,128)} %bitcast.1), calls=%async_computation.1 | async-start | bytes 131072 | tf_op jit(solution)/shard_map/all_to_all | solution.py:257
  30.0 0.7 %collective-permute-start.2 = (f32[8,512]{1,0:T(8,128)S(1)}, f32[8,512]{1,0:T(8,128)S(1)}, u32[]{:S(2)}, u32[]{:S(2)}) collective-permute-start(f32[8,512]{1,0:T(8,128)S(1)} %get-tuple-element.18), channel_id=1, source_target_pairs={{8,264},{12,268},{16,272},{20,276},{24,280},{28,284},{32,288},{36,... | collective-permute-start | bytes 49160 | tf_op jit(solution)/shard_map/ppermute | solution.py:249
  30.6 4.4 %collective-permute-start.1 = (f32[8,512]{1,0:T(8,128)S(1)}, f32[8,512]{1,0:T(8,128)S(1)}, u32[]{:S(2)}, u32[]{:S(2)}) collective-permute-start(f32[8,512]{1,0:T(8,128)S(1)} %get-tuple-element.18), channel_id=1, source_target_pairs={{0,256},{4,260},{64,320},{68,324},{128,384},{132,388},{192,448},{1... | collective-permute-start | bytes 49160 | tf_op jit(solution)/shard_map/ppermute | solution.py:248
  35.1 0.0 collective-permute-done.2.late_ref
  35.1 3.9 %collective-permute-done.1.far_ref = f32[8,512]{1,0:T(8,128)S(1)} collective-permute-done((f32[8,512]{1,0:T(8,128)S(1)}, f32[8,512]{1,0:T(8,128)S(1)}, u32[]{:S(2)}, u32[]{:S(2)}) %collective-permute-start.1) | collective-permute-done | bytes 16416 | tf_op jit(solution)/shard_map/ppermute | solution.py:248
  39.0 0.0 all-to-all-done.1
  39.0 0.3 filter_tiles.1
  39.3 17.2 %all_to_all.22 = f32[128,1,128]{2,1,0:T(1,128)S(1)} all-to-all(f32[128,1,128]{2,1,0:T(1,128)S(1)} %get-tuple-element.20), channel_id=1, replica_groups={{356,0,64,128,192,256,320,384,448,4,68,132,196,260,324,388,452,8,72,136..., dimensions={0} | all-to-all | bytes 131072 | tf_op jit(solution)/shard_map/all_to_all | solution.py:270
  56.5 0.1 fusion.1
  56.7 0.7 %subtract_multiply_fusion = f32[4,8,128]{2,1,0:T(8,128)} fusion(f32[4,8,128]{2,1,0:T(8,128)S(1)} %get-tuple-element.19, f32[4]{0:T(128)S(1)} %add_rsqrt_fusion, f32[4]{0:T(128)S(1)} %broadcast_multiply_fusion), kind=kLoop, calls=%fused_computation.4 | loop fusion | flops 8192 | bytes 32800 | tf_op jit(solution)/shard_map/mul | solution.py:277
  (3 shorter events, 0.0 us)
Async XLA Ops:
  9.3 14.9 %collective-permute-start = (f32[16,512]{1,0:T(8,128)S(1)}, f32[16,512]{1,0:T(8,128)S(1)}, u32[]{:S(2)}, u32[]{:S(2)}) collective-permute-start(f32[16,512]{1,0:T(8,128)S(1)} %get-tuple-element.17), channel_id=1, source_target_pairs={{0,504},{4,508},{8,16},{12,20},{16,8},{20,12},{24,32},{28,36},{32,... | collective-permute-start | bytes 98312 | tf_op jit(solution)/shard_map/ppermute | solution.py:250
  24.8 14.3 %all-to-all-start.1 = ((f32[4,8,512]{2,1,0:T(8,128)}), f32[4,8,512]{2,1,0:T(8,128)S(1)}, u32[]{:S(2)}, u32[]{:S(2)}) async-start(f32[4,8,512]{2,1,0:T(8,128)} %bitcast.1), calls=%async_computation.1 | async-start | bytes 131072 | tf_op jit(solution)/shard_map/all_to_all | solution.py:257
  30.0 5.1 %collective-permute-start.2 = (f32[8,512]{1,0:T(8,128)S(1)}, f32[8,512]{1,0:T(8,128)S(1)}, u32[]{:S(2)}, u32[]{:S(2)}) collective-permute-start(f32[8,512]{1,0:T(8,128)S(1)} %get-tuple-element.18), channel_id=1, source_target_pairs={{8,264},{12,268},{16,272},{20,276},{24,280},{28,284},{32,288},{36,... | collective-permute-start | bytes 49160 | tf_op jit(solution)/shard_map/ppermute | solution.py:249
  30.6 8.4 %collective-permute-start.1 = (f32[8,512]{1,0:T(8,128)S(1)}, f32[8,512]{1,0:T(8,128)S(1)}, u32[]{:S(2)}, u32[]{:S(2)}) collective-permute-start(f32[8,512]{1,0:T(8,128)S(1)} %get-tuple-element.18), channel_id=1, source_target_pairs={{0,256},{4,260},{64,320},{68,324},{128,384},{132,388},{192,448},{1... | collective-permute-start | bytes 49160 | tf_op jit(solution)/shard_map/ppermute | solution.py:248

commit v5 on v4

--- a/solution.py
+++ b/solution.py
@@ -11,7 +11,7 @@
 GROUP = 4
 CROSS = 2
 ROW = 16
-EARLY = 2
+EARLY = 4
 LEV_FIRST = 2
 NEAR_FIRST = 3
 STATS_FIRST = 89
@@ -187,7 +187,7 @@
         off = y - mean
         spread = jnp.sum(jnp.sum(off * off, axis=0, keepdims=True), axis=1, keepdims=True)
         stats = jnp.where(lane == r, mean, jnp.where(lane == rows + r, spread, stats))
-    stats_ref[...] = jnp.broadcast_to(stats[None], stats_ref.shape)
+    stats_ref[...] = jnp.broadcast_to(stats, stats_ref.shape)
 
 
 def remap_step(fields, bracket, fraction, remap_weights, intersections, tile_owner):
@@ -260,13 +260,14 @@
         filter_kernel,
         out_shape=[
             jax.ShapeDtypeStruct((rows, tile_dev, tile_cells), f32),
-            jax.ShapeDtypeStruct((col_count, 1, tile_cells), f32),
+            jax.ShapeDtypeStruct((col_count, tile_cells), f32),
         ],
         name="filter_tiles",
         compiler_params=PARAMS,
     )(near, far_a, far_b)
     lead = STATS_FIRST
     order = sorted(range(col_count), key=lambda d: (d != lead, d % ROW, d))
+    stats = stats.reshape(col_count, 1, tile_cells)
     stats = lax.all_to_all(stats, "col", 0, 0, tiled=True, axis_index_groups=[order])[:, 0]
     count = float(tile_dev * tile_cells)
     field_mean = jnp.sum(stats[:, :rows], axis=0) / float(col_count)

time: 57.7 us -> 57.9 us (level)
  no operation moved by 1% of the time
where the time goes in v5:
time: 57.9 us; the launch traced here: 57.6 us
  blocking collectives  24.8 us (43%)
  starting transfers between devices  23.9 us (41%)
  waiting for transfers between devices  5.23 us (9%)
  Pallas kernels  2.5 us (4%)
  other arithmetic  1.01 us (2%)
    all_to_all x1, blocking collectives, remap_step(): lax.all_to_all(stats, 'col', 0, 0, tiled=True, axis_index_groups=[order])  17.2 us
    ppermute x1, starting transfers between devices, remap_step(): cross = lax.ppermute(cross, 'col', swap)  13.6 us
    all_to_all x1, blocking collectives, remap_step(): lax.all_to_all(mixed, 'lev', 0, 0, tiled=True, axis_index_groups=levs)  7.62 us
    all_to_all x1, starting transfers between devices, remap_step(): lax.all_to_all(near, 'col', 0, 0, tiled=True, axis_index_groups=groups)  5.23 us
    ppermute x1, starting transfers between devices, remap_step(): far_a = lax.ppermute(far, 'col', early)  4.43 us
    ppermute x1, waiting for transfers between devices, remap_step(): far_a = lax.ppermute(far, 'col', early)  3.94 us
    ppermute x1, waiting for transfers between devices, remap_step(): cross = lax.ppermute(cross, 'col', swap)  1.29 us
    pallas_call x1, Pallas kernels, remap_step(): pl.pallas_call(prepare_kernel, in_specs=[anywhere] * 6, out_shape=[jax.Sh...  1.2 us
  transfers between devices with their start and end apart: 4, of which 2 were waited for; matrix products, arithmetic and copies ran while one was open for 0% of the time, Pallas kernels for 0%

profile of v5, /device:TPU:1, one launch (start us, length us, event | category | flops | bytes accessed | tf_op | source)
XLA Modules:
  0.0 57.6 jit_solution(4601577235774638338)
XLA Ops:
  0.0 1.2 %mix_and_count.1 = (f32[4,4,8,128]{3,2,1,0:T(8,128)S(1)}, f32[56,128]{1,0:T(8,128)S(1)}, bf16[16,128,128]{2,1,0:T(8,128)(2,1)S(1)}) custom-call(bf16[2,8,1024]{2,1,0:T(8,128)(2,1)} %fields_hbm.1, s32[8,1024]{1,0:T(8,128)} %bracket_hbm.1, f32[8,1024]{1,0:T(8,128)} %fraction_hbm.1, s32[3,32]{1,0:T(4,128)} %intersections_hbm.1, s32[8,128]{1,0:T(8,128)} %bitcast.12, ...), custom_call_target="tpu_custom_call" | custom-call | tf_op jit(solution)/shard_map/mix_and_count/pallas_call | solution.py:208
  1.2 7.6 %all_to_all.21.mixed_ref = f32[4,4,8,128]{3,2,1,0:T(8,128)S(1)} all-to-all(f32[4,4,8,128]{3,2,1,0:T(8,128)S(1)} %get-tuple-element.13), channel_id=1, replica_groups={{2,3,0,1},{6,7,4,5},{10,11,8,9},{14,15,12,13},{18,19,16,17},{22,23,20,2..., dimensions={0} | all-to-all | bytes 131072 | tf_op jit(solution)/shard_map/all_to_all | solution.py:228
  8.8 0.4 remap_blocks.1
  9.3 13.6 %collective-permute-start = (f32[16,512]{1,0:T(8,128)S(1)}, f32[16,512]{1,0:T(8,128)S(1)}, u32[]{:S(2)}, u32[]{:S(2)}) collective-permute-start(f32[16,512]{1,0:T(8,128)S(1)} %get-tuple-element.17), channel_id=1, source_target_pairs={{0,504},{4,508},{8,16},{12,20},{16,8},{20,12},{24,32},{28,36},{32,... | collective-permute-start | bytes 98312 | tf_op jit(solution)/shard_map/ppermute | solution.py:250
  22.8 1.3 %collective-permute-done.cross_ref = f32[16,512]{1,0:T(8,128)S(1)} collective-permute-done((f32[16,512]{1,0:T(8,128)S(1)}, f32[16,512]{1,0:T(8,128)S(1)}, u32[]{:S(2)}, u32[]{:S(2)}) %collective-permute-start) | collective-permute-done | bytes 32800 | tf_op jit(solution)/shard_map/ppermute | solution.py:250
  24.1 0.6 %join_forwarded.1 = f32[32,512]{1,0:T(8,128)} custom-call(f32[32,512]{1,0:T(8,128)S(1)} %get-tuple-element.16.group_ref, f32[16,512]{1,0:T(8,128)S(1)} %collective-permute-done.cross_ref), custom_call_target="tpu_custom_call" | custom-call | tf_op jit(solution)/shard_map/join_forwarded/pallas_call | solution.py:251
  24.8 5.2 %all-to-all-start.1 = ((f32[4,8,512]{2,1,0:T(8,128)}), f32[4,8,512]{2,1,0:T(8,128)S(1)}, u32[]{:S(2)}, u32[]{:S(2)}) async-start(f32[4,8,512]{2,1,0:T(8,128)} %bitcast.1), calls=%async_computation.1 | async-start | bytes 131072 | tf_op jit(solution)/shard_map/all_to_all | solution.py:257
  30.0 0.7 %collective-permute-start.2 = (f32[8,512]{1,0:T(8,128)S(1)}, f32[8,512]{1,0:T(8,128)S(1)}, u32[]{:S(2)}, u32[]{:S(2)}) collective-permute-start(f32[8,512]{1,0:T(8,128)S(1)} %get-tuple-element.18), channel_id=1, source_target_pairs={{16,272},{20,276},{24,280},{28,284},{32,288},{36,292},{40,296},{44... | collective-permute-start | bytes 49160 | tf_op jit(solution)/shard_map/ppermute | solution.py:249
  30.6 4.4 %collective-permute-start.1 = (f32[8,512]{1,0:T(8,128)S(1)}, f32[8,512]{1,0:T(8,128)S(1)}, u32[]{:S(2)}, u32[]{:S(2)}) collective-permute-start(f32[8,512]{1,0:T(8,128)S(1)} %get-tuple-element.18), channel_id=1, source_target_pairs={{0,256},{4,260},{8,264},{12,268},{64,320},{68,324},{72,328},{76,33... | collective-permute-start | bytes 49160 | tf_op jit(solution)/shard_map/ppermute | solution.py:248
  35.1 0.0 collective-permute-done.2.late_ref
  35.1 3.9 %collective-permute-done.1.far_ref = f32[8,512]{1,0:T(8,128)S(1)} collective-permute-done((f32[8,512]{1,0:T(8,128)S(1)}, f32[8,512]{1,0:T(8,128)S(1)}, u32[]{:S(2)}, u32[]{:S(2)}) %collective-permute-start.1) | collective-permute-done | bytes 16416 | tf_op jit(solution)/shard_map/ppermute | solution.py:248
  39.0 0.0 all-to-all-done.1
  39.0 0.3 filter_tiles.1
  39.3 17.2 %all_to_all.22 = f32[128,1,128]{2,1,0:T(1,128)S(1)} all-to-all(f32[128,1,128]{2,1,0:T(1,128)S(1)} %bitcast.9), channel_id=1, replica_groups={{356,0,64,128,192,256,320,384,448,4,68,132,196,260,324,388,452,8,72,136..., dimensions={0} | all-to-all | bytes 131072 | tf_op jit(solution)/shard_map/all_to_all | solution.py:271
  56.5 0.1 copy.9
  56.6 0.1 slice_reduce_fusion
  56.7 0.2 fusion.1
  56.9 0.7 %subtract_multiply_fusion = f32[4,8,128]{2,1,0:T(8,128)} fusion(f32[4,8,128]{2,1,0:T(8,128)S(1)} %get-tuple-element.19, f32[4]{0:T(128)S(1)} %add_rsqrt_fusion, f32[4]{0:T(128)S(1)} %broadcast_multiply_fusion), kind=kLoop, calls=%fused_computation | loop fusion | flops 8192 | bytes 32800 | tf_op jit(solution)/shard_map/mul | solution.py:278
  (2 shorter events, 0.0 us)
Async XLA Ops:
  9.3 14.9 %collective-permute-start = (f32[16,512]{1,0:T(8,128)S(1)}, f32[16,512]{1,0:T(8,128)S(1)}, u32[]{:S(2)}, u32[]{:S(2)}) collective-permute-start(f32[16,512]{1,0:T(8,128)S(1)} %get-tuple-element.17), channel_id=1, source_target_pairs={{0,504},{4,508},{8,16},{12,20},{16,8},{20,12},{24,32},{28,36},{32,... | collective-permute-start | bytes 98312 | tf_op jit(solution)/shard_map/ppermute | solution.py:250
  24.8 14.3 %all-to-all-start.1 = ((f32[4,8,512]{2,1,0:T(8,128)}), f32[4,8,512]{2,1,0:T(8,128)S(1)}, u32[]{:S(2)}, u32[]{:S(2)}) async-start(f32[4,8,512]{2,1,0:T(8,128)} %bitcast.1), calls=%async_computation.1 | async-start | bytes 131072 | tf_op jit(solution)/shard_map/all_to_all | solution.py:257
  30.0 5.1 %collective-permute-start.2 = (f32[8,512]{1,0:T(8,128)S(1)}, f32[8,512]{1,0:T(8,128)S(1)}, u32[]{:S(2)}, u32[]{:S(2)}) collective-permute-start(f32[8,512]{1,0:T(8,128)S(1)} %get-tuple-element.18), channel_id=1, source_target_pairs={{16,272},{20,276},{24,280},{28,284},{32,288},{36,292},{40,296},{44... | collective-permute-start | bytes 49160 | tf_op jit(solution)/shard_map/ppermute | solution.py:249
  30.6 8.4 %collective-permute-start.1 = (f32[8,512]{1,0:T(8,128)S(1)}, f32[8,512]{1,0:T(8,128)S(1)}, u32[]{:S(2)}, u32[]{:S(2)}) collective-permute-start(f32[8,512]{1,0:T(8,128)S(1)} %get-tuple-element.18), channel_id=1, source_target_pairs={{0,256},{4,260},{8,264},{12,268},{64,320},{68,324},{72,328},{76,33... | collective-permute-start | bytes 49160 | tf_op jit(solution)/shard_map/ppermute | solution.py:248

commit v6 on v5

--- a/solution.py
+++ b/solution.py
@@ -11,7 +11,7 @@
 GROUP = 4
 CROSS = 2
 ROW = 16
-EARLY = 4
+EARLY = 2
 LEV_FIRST = 2
 NEAR_FIRST = 3
 STATS_FIRST = 89
@@ -190,6 +190,21 @@
     stats_ref[...] = jnp.broadcast_to(stats, stats_ref.shape)
 
 
+def normalize_kernel(stats_ref, filtered_ref, out_ref):
+    rows, tile_dev, cells = filtered_ref.shape
+    devices = stats_ref.shape[0]
+    count = float(tile_dev * cells)
+    stats = stats_ref[...]
+    mean = jnp.sum(stats, axis=0, keepdims=True) / float(devices)
+    apart = stats - mean
+    between = jnp.sum(apart * apart, axis=0, keepdims=True)
+    within = mean * float(devices)
+    for r in range(rows):
+        spread = within[:, rows + r : rows + r + 1] + count * between[:, r : r + 1]
+        scale = lax.rsqrt(spread / (count * float(devices)) + epsilon)
+        out_ref[r] = (filtered_ref[r] - mean[:, r : r + 1]) * scale
+
+
 def remap_step(fields, bracket, fraction, remap_weights, intersections, tile_owner):
     lev_dev = lax.axis_size("lev")
     col_count = lax.axis_size("col")
@@ -268,14 +283,13 @@
     lead = STATS_FIRST
     order = sorted(range(col_count), key=lambda d: (d != lead, d % ROW, d))
     stats = stats.reshape(col_count, 1, tile_cells)
-    stats = lax.all_to_all(stats, "col", 0, 0, tiled=True, axis_index_groups=[order])[:, 0]
-    count = float(tile_dev * tile_cells)
-    field_mean = jnp.sum(stats[:, :rows], axis=0) / float(col_count)
-    apart = stats[:, :rows] - field_mean[None]
-    spread = jnp.sum(stats[:, rows : 2 * rows] + count * apart * apart, axis=0)
-    field_var = spread / (count * col_count)
-    scale = lax.rsqrt(field_var + epsilon)
-    normalized = (filtered - field_mean[:, None, None]) * scale[:, None, None]
+    stats = lax.all_to_all(stats, "col", 0, 0, tiled=True, axis_index_groups=[order])
+    normalized = pl.pallas_call(
+        normalize_kernel,
+        out_shape=jax.ShapeDtypeStruct(filtered.shape, f32),
+        name="normalize_tiles",
+        compiler_params=PARAMS,
+    )(stats.reshape(col_count, tile_cells), filtered)
     return normalized.reshape(F, plev_dev, tile_dev, tile_cells)
 
 

time: 57.9 us -> 57.7 us (level)
  other arithmetic: 1.01 us -> 0 us
  Pallas kernels: 2.5 us -> 3.34 us
    pallas_call x0 -> x1, Pallas kernels: none -> 0.84 us  [remap_step(): pl.pallas_call(normalize_kernel, out_shape=jax.ShapeDtypeStruct(filtered....]
    mul x1 -> x0, other arithmetic: 0.69 us -> none  [remap_step(): normalized = (filtered - field_mean[:, None, None]) * scale[:, None, None]]
where the time goes in v6:
time: 57.7 us; the launch traced here: 57.3 us
  blocking collectives  24.8 us (43%)
  starting transfers between devices  23.9 us (41%)
  waiting for transfers between devices  5.23 us (9%)
  Pallas kernels  3.34 us (6%)
    all_to_all x1, blocking collectives, remap_step(): lax.all_to_all(stats, 'col', 0, 0, tiled=True, axis_index_groups=[order])  17.2 us
    ppermute x1, starting transfers between devices, remap_step(): cross = lax.ppermute(cross, 'col', swap)  13.6 us
    all_to_all x1, blocking collectives, remap_step(): lax.all_to_all(mixed, 'lev', 0, 0, tiled=True, axis_index_groups=levs)  7.62 us
    all_to_all x1, starting transfers between devices, remap_step(): lax.all_to_all(near, 'col', 0, 0, tiled=True, axis_index_groups=groups)  5.23 us
    ppermute x1, starting transfers between devices, remap_step(): far_a = lax.ppermute(far, 'col', early)  4.43 us
    ppermute x1, waiting for transfers between devices, remap_step(): far_a = lax.ppermute(far, 'col', early)  3.94 us
    ppermute x1, waiting for transfers between devices, remap_step(): cross = lax.ppermute(cross, 'col', swap)  1.29 us
    pallas_call x1, Pallas kernels, remap_step(): pl.pallas_call(prepare_kernel, in_specs=[anywhere] * 6, out_shape=[jax.Sh...  1.2 us
  transfers between devices with their start and end apart: 4, of which 2 were waited for; matrix products, arithmetic and copies ran while one was open for 0% of the time, Pallas kernels for 0%

profile of v6, /device:TPU:1, one launch (start us, length us, event | category | flops | bytes accessed | tf_op | source)
XLA Modules:
  0.0 57.3 jit_solution(10967290237350273091)
XLA Ops:
  0.0 1.2 %mix_and_count.1 = (f32[4,4,8,128]{3,2,1,0:T(8,128)S(1)}, f32[56,128]{1,0:T(8,128)S(1)}, bf16[16,128,128]{2,1,0:T(8,128)(2,1)S(1)}) custom-call(bf16[2,8,1024]{2,1,0:T(8,128)(2,1)} %fields_hbm.1, s32[8,1024]{1,0:T(8,128)} %bracket_hbm.1, f32[8,1024]{1,0:T(8,128)} %fraction_hbm.1, s32[3,32]{1,0:T(4,128)} %intersections_hbm.1, s32[8,128]{1,0:T(8,128)} %bitcast.11, ...), custom_call_target="tpu_custom_call" | custom-call | tf_op jit(solution)/shard_map/mix_and_count/pallas_call | solution.py:223
  1.2 7.6 %all_to_all.21.mixed_ref = f32[4,4,8,128]{3,2,1,0:T(8,128)S(1)} all-to-all(f32[4,4,8,128]{3,2,1,0:T(8,128)S(1)} %get-tuple-element.13), channel_id=1, replica_groups={{2,3,0,1},{6,7,4,5},{10,11,8,9},{14,15,12,13},{18,19,16,17},{22,23,20,2..., dimensions={0} | all-to-all | bytes 131072 | tf_op jit(solution)/shard_map/all_to_all | solution.py:243
  8.8 0.4 remap_blocks.1
  9.3 13.6 %collective-permute-start = (f32[16,512]{1,0:T(8,128)S(1)}, f32[16,512]{1,0:T(8,128)S(1)}, u32[]{:S(2)}, u32[]{:S(2)}) collective-permute-start(f32[16,512]{1,0:T(8,128)S(1)} %get-tuple-element.17), channel_id=1, source_target_pairs={{0,504},{4,508},{8,16},{12,20},{16,8},{20,12},{24,32},{28,36},{32,... | collective-permute-start | bytes 98312 | tf_op jit(solution)/shard_map/ppermute | solution.py:265
  22.8 1.3 %collective-permute-done.cross_ref = f32[16,512]{1,0:T(8,128)S(1)} collective-permute-done((f32[16,512]{1,0:T(8,128)S(1)}, f32[16,512]{1,0:T(8,128)S(1)}, u32[]{:S(2)}, u32[]{:S(2)}) %collective-permute-start) | collective-permute-done | bytes 32800 | tf_op jit(solution)/shard_map/ppermute | solution.py:265
  24.1 0.6 %join_forwarded.1 = f32[32,512]{1,0:T(8,128)} custom-call(f32[32,512]{1,0:T(8,128)S(1)} %get-tuple-element.16.group_ref, f32[16,512]{1,0:T(8,128)S(1)} %collective-permute-done.cross_ref), custom_call_target="tpu_custom_call" | custom-call | tf_op jit(solution)/shard_map/join_forwarded/pallas_call | solution.py:266
  24.8 5.2 %all-to-all-start.1 = ((f32[4,8,512]{2,1,0:T(8,128)}), f32[4,8,512]{2,1,0:T(8,128)S(1)}, u32[]{:S(2)}, u32[]{:S(2)}) async-start(f32[4,8,512]{2,1,0:T(8,128)} %bitcast.1), calls=%async_computation.1 | async-start | bytes 131072 | tf_op jit(solution)/shard_map/all_to_all | solution.py:272
  30.0 0.7 %collective-permute-start.2 = (f32[8,512]{1,0:T(8,128)S(1)}, f32[8,512]{1,0:T(8,128)S(1)}, u32[]{:S(2)}, u32[]{:S(2)}) collective-permute-start(f32[8,512]{1,0:T(8,128)S(1)} %get-tuple-element.18), channel_id=1, source_target_pairs={{8,264},{12,268},{16,272},{20,276},{24,280},{28,284},{32,288},{36,... | collective-permute-start | bytes 49160 | tf_op jit(solution)/shard_map/ppermute | solution.py:264
  30.7 4.4 %collective-permute-start.1 = (f32[8,512]{1,0:T(8,128)S(1)}, f32[8,512]{1,0:T(8,128)S(1)}, u32[]{:S(2)}, u32[]{:S(2)}) collective-permute-start(f32[8,512]{1,0:T(8,128)S(1)} %get-tuple-element.18), channel_id=1, source_target_pairs={{0,256},{4,260},{64,320},{68,324},{128,384},{132,388},{192,448},{1... | collective-permute-start | bytes 49160 | tf_op jit(solution)/shard_map/ppermute | solution.py:263
  35.1 0.0 collective-permute-done.2.late_ref
  35.1 3.9 %collective-permute-done.1.far_ref = f32[8,512]{1,0:T(8,128)S(1)} collective-permute-done((f32[8,512]{1,0:T(8,128)S(1)}, f32[8,512]{1,0:T(8,128)S(1)}, u32[]{:S(2)}, u32[]{:S(2)}) %collective-permute-start.1) | collective-permute-done | bytes 16416 | tf_op jit(solution)/shard_map/ppermute | solution.py:263
  39.0 0.0 all-to-all-done.1
  39.0 0.3 filter_tiles.1
  39.3 17.2 %all_to_all.22 = f32[128,1,128]{2,1,0:T(1,128)S(1)} all-to-all(f32[128,1,128]{2,1,0:T(1,128)S(1)} %bitcast.10), channel_id=1, replica_groups={{356,0,64,128,192,256,320,384,448,4,68,132,196,260,324,388,452,8,72,136..., dimensions={0} | all-to-all | bytes 131072 | tf_op jit(solution)/shard_map/all_to_all | solution.py:286
  56.5 0.8 %normalize_tiles.1 = f32[4,8,128]{2,1,0:T(8,128)} custom-call(f32[128,128]{1,0:T(8,128)S(1)} %bitcast.9, f32[4,8,128]{2,1,0:T(8,128)S(1)} %get-tuple-element.20.filtered_ref), custom_call_target="tpu_custom_call" | custom-call | tf_op jit(solution)/shard_map/normalize_tiles/pallas_call | solution.py:287
Async XLA Ops:
  9.3 14.9 %collective-permute-start = (f32[16,512]{1,0:T(8,128)S(1)}, f32[16,512]{1,0:T(8,128)S(1)}, u32[]{:S(2)}, u32[]{:S(2)}) collective-permute-start(f32[16,512]{1,0:T(8,128)S(1)} %get-tuple-element.17), channel_id=1, source_target_pairs={{0,504},{4,508},{8,16},{12,20},{16,8},{20,12},{24,32},{28,36},{32,... | collective-permute-start | bytes 98312 | tf_op jit(solution)/shard_map/ppermute | solution.py:265
  24.8 14.3 %all-to-all-start.1 = ((f32[4,8,512]{2,1,0:T(8,128)}), f32[4,8,512]{2,1,0:T(8,128)S(1)}, u32[]{:S(2)}, u32[]{:S(2)}) async-start(f32[4,8,512]{2,1,0:T(8,128)} %bitcast.1), calls=%async_computation.1 | async-start | bytes 131072 | tf_op jit(solution)/shard_map/all_to_all | solution.py:272
  30.0 5.1 %collective-permute-start.2 = (f32[8,512]{1,0:T(8,128)S(1)}, f32[8,512]{1,0:T(8,128)S(1)}, u32[]{:S(2)}, u32[]{:S(2)}) collective-permute-start(f32[8,512]{1,0:T(8,128)S(1)} %get-tuple-element.18), channel_id=1, source_target_pairs={{8,264},{12,268},{16,272},{20,276},{24,280},{28,284},{32,288},{36,... | collective-permute-start | bytes 49160 | tf_op jit(solution)/shard_map/ppermute | solution.py:264
  30.7 8.4 %collective-permute-start.1 = (f32[8,512]{1,0:T(8,128)S(1)}, f32[8,512]{1,0:T(8,128)S(1)}, u32[]{:S(2)}, u32[]{:S(2)}) collective-permute-start(f32[8,512]{1,0:T(8,128)S(1)} %get-tuple-element.18), channel_id=1, source_target_pairs={{0,256},{4,260},{64,320},{68,324},{128,384},{132,388},{192,448},{1... | collective-permute-start | bytes 49160 | tf_op jit(solution)/shard_map/ppermute | solution.py:263
